TPU v7x, 32 devices: a whole 2x2x4 slice. The times are simulated.
32 devices in a mesh: row: 8 (over y, x, core), col: 4 (over z).
Axes of the slice: x: 2, y: 2, z: 4, core: 2. Of those that a mesh axis runs over, the one named last changes fastest.
Arguments:
- amplitudes: bfloat16 [24576, 24576], P('col', 'row'), may hold values from -0.0390625 to 0.0390625
- cholesky: bfloat16 [24576, 1280], P(('row', 'col')), may hold values from -5 to 5
- occ_map: int32 [24576], replicated, may hold values from 0 to 47
- vir_map: int32 [24576], replicated, may hold values from 0 to 511
Outputs:
- new_amplitudes: bfloat16 [24576, 24576], P('col', 'row')
All inputs are finite; a program needn't handle non-finite values.
Results may differ from a plain program's by a relative error of at most 0.0056.
Values may be sent and summed in bfloat16 or wider, within the bound.
No kernel may reach another device: no remote copies, remote signals or barrier semaphores. Data moves between devices by JAX's collectives and lax.ppermute only.
A program may use at most 192 MiB of HBM per device.

v0:
```python
import jax
import jax.numpy as jnp
from jax import lax
from jax.sharding import PartitionSpec as P

NOCC = 48
NVIR = 512


def broadcast(x, axis, root):
    mine = lax.axis_index(axis) == root
    return lax.psum(jnp.where(mine, x, jnp.zeros_like(x)), axis)


def pair_gap(occ_map, vir_map):
    occ = occ_map.astype(jnp.float32)
    vir = vir_map.astype(jnp.float32)
    return 0.5 + 2.5 * jnp.sqrt(vir / NVIR) + (0.5 + 2.5 * occ / NOCC)


def body(amplitudes, cholesky, occ_map, vir_map):
    tile_rows, tile_cols = amplitudes.shape
    row_index = lax.axis_index("row")
    col_index = lax.axis_index("col")
    q_start = row_index * tile_cols
    p_start = col_index * tile_rows
    offset = q_start - p_start
    on_diag = jnp.logical_and(offset >= 0, offset < tile_rows).astype(jnp.float32)
    safe_offset = jnp.clip(offset, 0, tile_rows - tile_cols)
    piece = lax.all_gather(cholesky, "col", axis=0, tiled=True)
    count = piece.shape[0]
    total = jnp.dot(amplitudes, piece, preferred_element_type=jnp.float32)
    current = lax.dynamic_slice_in_dim(total, safe_offset, count, 0)
    partial_value = lax.dynamic_update_slice_in_dim(
        total, current + on_diag * piece.astype(jnp.float32), safe_offset, 0
    )
    y_share = lax.psum_scatter(partial_value, "row", scatter_dimension=0, tiled=True).astype(
        jnp.bfloat16
    )
    y_block = lax.all_gather(y_share, "row", axis=0, tiled=True)
    q_root = q_start // tile_rows
    q_inside = q_start % tile_rows
    own_part = lax.dynamic_slice_in_dim(y_block, q_inside, tile_cols, 0)
    y_cols = broadcast(own_part, "col", q_root)
    cycle = lax.dot_general(
        y_block, y_cols, (((1,), (1,)), ((), ())), preferred_element_type=jnp.float32
    )
    gap_rows = pair_gap(
        lax.dynamic_slice_in_dim(occ_map, p_start, tile_rows, 0),
        lax.dynamic_slice_in_dim(vir_map, p_start, tile_rows, 0),
    )
    gap_cols = pair_gap(
        lax.dynamic_slice_in_dim(occ_map, q_start, tile_cols, 0),
        lax.dynamic_slice_in_dim(vir_map, q_start, tile_cols, 0),
    )
    return (-cycle / (gap_rows[:, None] + gap_cols[None, :])).astype(jnp.bfloat16)


def solution(mesh):
    return jax.shard_map(
        body,
        mesh=mesh,
        in_specs=(P("col", "row"), P(("row", "col"), None), P(), P()),
        out_specs=P("col", "row"),
        check_vma=False,
    )
```

profile of v0, /device:TPU:0, one launch (start us, length us, event | category | flops | bytes accessed | tf_op | source)
XLA Modules:
  0.0 884.4 jit_solution(14098019015922236109)
XLA Ops:
  6.5 0.0 all-gather.3.cloned.1.call-start
  6.5 0.7 all-gather.3.cloned.1.call-update
  7.3 0.0 reduce-scatter.2.cloned.1.call-start
  7.3 145.4 %all-gather.3.cloned.1.call-done = bf16[3072,1280]{1,0:T(8,128)(2,1)} async-done(((bf16[768,1280]{1,0:T(8,128)(2,1)}), bf16[3072,1280]{1,0:T(8,128)(2,1)}) %all-gather.3.cloned.1.call-update) | async-done | bytes 7864336 | tf_op jit(solution)/shard_map/all_gather | solution.py:30
  152.7 0.0 copy-start
  152.7 58.6 %fusion = f32[6144,1280]{1,0:T(8,128)} fusion(bf16[6144,3072]{1,0:T(8,128)(2,1)} %param.4, bf16[3072,1280]{1,0:T(8,128)(2,1)} %all-gather.3.cloned.1.call-done), kind=kOutput, calls=%fused_computation.5 | convolution fusion | flops 48318382080 | bytes 77070336 | tf_op jit(solution)/shard_map/dot_general | solution.py:32
  211.3 0.0 copy-done
  211.3 11.6 %multiply_add_fusion = f32[3072,1280]{1,0:T(8,128)} fusion(bf16[3072,1280]{1,0:T(8,128)(2,1)S(1)} %copy-done, f32[6144,1280]{1,0:T(8,128)} %fusion, s32[]{:T(128)S(6)} %min.4, f32[]{:T(128)S(6)} %convert_element_type.24), kind=kLoop, calls=%fused_computation.1 | loop fusion | flops 11796480 | bytes 39321608 | tf_op jit(solution)/shard_map/add | solution.py:35
  222.9 36.3 %dynamic_update_slice.3 = f32[6144,1280]{1,0:T(8,128)} dynamic-update-slice(f32[6144,1280]{1,0:T(8,128)} %fusion, f32[3072,1280]{1,0:T(8,128)} %multiply_add_fusion, s32[]{:T(128)S(6)} %min.4, s32[]{:T(128)} %constant.40.clone.1) | dynamic-update-slice | bytes 31457284 | tf_op jit(solution)/shard_map/dynamic_update_slice | solution.py:34
  259.2 0.0 reduce-scatter.2.cloned.1.call-update
  259.2 0.0 all-gather.5.cloned.1.call-start
  259.3 190.0 %reduce-scatter.2.cloned.1.call-done = f32[768,1280]{1,0:T(8,128)} async-done(((f32[6144,1280]{1,0:T(8,128)}), f32[768,1280]{1,0:T(8,128)}) %reduce-scatter.2.cloned.1.call-update) | async-done | bytes 3932176 | tf_op jit(solution)/shard_map/reduce_scatter | solution.py:37
  449.3 3.6 convert_element_type.26
  452.8 0.0 all-gather.5.cloned.1.call-update
  452.9 0.2 all-reduce.2.cloned.1.call-start
  453.1 85.2 %all-gather.5.cloned.1.call-done = bf16[6144,1280]{1,0:T(8,128)(2,1)} async-done(((bf16[768,1280]{1,0:T(8,128)(2,1)}), bf16[6144,1280]{1,0:T(8,128)(2,1)}) %all-gather.5.cloned.1.call-update) | async-done | bytes 15728656 | tf_op jit(solution)/shard_map/all_gather | solution.py:40
  538.3 8.8 dynamic-slice_select_fusion
  547.2 0.0 all-reduce.2.cloned.1.call-update
  547.2 0.7 add_add_fusion.1
  547.9 0.8 add_add_fusion
  548.7 272.4 %all-reduce.2.cloned.1.call-done = bf16[3072,1280]{1,0:T(8,128)(2,1)} async-done(((bf16[3072,1280]{1,0:T(8,128)(2,1)}), bf16[3072,1280]{1,0:T(8,128)(2,1)}) %all-reduce.2.cloned.1.call-update) | async-done | bytes 7864336 | tf_op jit(solution)/shard_map/psum | solution.py:12
  821.1 56.7 %divide_convert_fusion = bf16[6144,3072]{1,0:T(8,128)(2,1)} fusion(bf16[6144,1280]{1,0:T(8,128)(2,1)} %all-gather.5.cloned.1.call-done, bf16[3072,1280]{1,0:T(8,128)(2,1)} %all-reduce.2.cloned.1.call-done, f32[3072]{0:T(1024)S(1)} %add_add_fusion.1, f32[6144]{0:T(1024)S(1)} %add_add_fusion), kind=kOutput, calls=%fused_computation | convolution fusion | flops 48393879552 | bytes 61378560 | tf_op jit(solution)/shard_map/dot_general | solution.py:45
Async XLA Ops:
  6.5 146.2 %all-gather.3.cloned.1.call-start = ((), (), s32[]{:S(2)}) async-start(), calls=%async_computation.1 | async-start | bytes 9830400 | tf_op jit(solution)/shard_map/all_gather | solution.py:30
  7.3 442.0 %reduce-scatter.2.cloned.1.call-start = ((), (), s32[]{:S(2)}) async-start(), calls=%async_computation.2 | async-start | bytes 35389440 | tf_op jit(solution)/shard_map/reduce_scatter | solution.py:37
  152.7 58.6 %copy-start = (bf16[3072,1280]{1,0:T(8,128)(2,1)S(1)}, bf16[3072,1280]{1,0:T(8,128)(2,1)}, u32[]{:S(2)}) copy-start(bf16[3072,1280]{1,0:T(8,128)(2,1)} %all-gather.3.cloned.1.call-done) | copy-start | bytes 23592964
  259.2 279.1 %all-gather.5.cloned.1.call-start = ((), (), s32[]{:S(2)}) async-start(), calls=%async_computation.3 | async-start | bytes 17694720 | tf_op jit(solution)/shard_map/all_gather | solution.py:40
  452.9 368.2 %all-reduce.2.cloned.1.call-start = ((), (), s32[]{:S(2)}) async-start(), calls=%async_computation.4 | async-start | bytes 15728640 | tf_op jit(solution)/shard_map/psum | solution.py:12
Sparse Core Ops, SparseCore 0:
  8.9 143.7 all-gather.2
  259.4 189.8 reduce-scatter.1
  453.0 85.3 all-gather.4
  547.3 273.7 all-reduce.1
where the time goes:
time: 886 us; the launch traced here: 884 us
  waiting for transfers between devices  694 us (78%)
  matrix products  115 us (13%)
  local copies, waits for them, and re-layouts  36.3 us (4%)
  other arithmetic  25.5 us (3%)
  between operations  13.2 us (1%)
    psum x1, waiting for transfers between devices, broadcast(): return lax.psum(jnp.where(mine, x, jnp.zeros_like(x)), axis)  272 us
    reduce_scatter x1, waiting for transfers between devices, body(): lax.psum_scatter(partial_value, 'row', scatter_dimension=0, tiled=True)  190 us
    all_gather x1, waiting for transfers between devices, body(): piece = lax.all_gather(cholesky, 'col', axis=0, tiled=True)  145 us
    all_gather x1, waiting for transfers between devices, body(): y_block = lax.all_gather(y_share, 'row', axis=0, tiled=True)  85.2 us
    dot_general x1, matrix products, body(): total = jnp.dot(amplitudes, piece, preferred_element_type=jnp.float32)  58.6 us
    dot_general x1, matrix products, body(): lax.dot_general(y_block, y_cols, (((1,), (1,)), ((), ())), preferred_elem...  56.7 us
    dynamic_update_slice x1, local copies, waits for them, and re-layouts, body(): lax.dynamic_update_slice_in_dim(total, current + on_diag * piece.astype(j...  36.3 us
  transfers between devices with their start and end apart: 4, of which 4 were waited for; matrix products, arithmetic and copies ran while one was open for 0% of the time, Pallas kernels for 0%

commit v1 on v0

v1 whole, which is shorter than its diff:
```python
import functools

import jax
import jax.numpy as jnp
from jax import lax
from jax.experimental import pallas as pl
from jax.experimental.pallas import tpu as pltpu
from jax.sharding import PartitionSpec as P

NOCC = 48
NVIR = 512
LANES = 128
BF = jnp.bfloat16
F32 = jnp.float32


def pair_gap(occ_map, vir_map):
    occ = occ_map.astype(jnp.float32)
    vir = vir_map.astype(jnp.float32)
    return 0.5 + 2.5 * jnp.sqrt(vir / NVIR) + (0.5 + 2.5 * occ / NOCC)


def first_kernel(keep, spots, chips, t_ref, *refs):
    count = len(refs) - 2
    out_ref, held = refs[count], refs[count + 1]
    height = refs[0].shape[0]
    width = out_ref.shape[2]
    step, phase = pl.program_id(0), pl.program_id(1)
    count_in = t_ref.shape[0] // width

    @pl.when(jnp.logical_and(step == 0, phase == 0))
    def _():
        for n in range(count):

            @pl.when(spots[n] >= 0)
            def _(n=n):
                held[pl.ds(pl.multiple_of(spots[n], 32), height), :] = refs[n][...]

    total = jnp.dot(t_ref[...], held[...], preferred_element_type=jnp.float32)
    if keep:
        tall = count_in * width
        at = (step * pl.num_programs(1) + phase) * tall
        own = held[pl.ds(pl.multiple_of(at, 32), tall), :].astype(jnp.float32)
        total = total + jnp.where(spots[count] > 0, own, jnp.zeros_like(own))
    for n in range(count_in):
        out_ref[chips[phase * count_in + n], 0] = total[n * width : (n + 1) * width]


def first_product(amplitudes, pieces, spots, chips, layers, strips, keep):
    tile_rows, depth = amplitudes.shape
    wide = pieces[0].shape[1]
    tall = tile_rows // (2 * strips)
    width = tall // layers
    grid_spec = pltpu.PrefetchScalarGridSpec(
        num_scalar_prefetch=2,
        grid=(strips, 2),
        in_specs=[
            pl.BlockSpec((tall // 2, depth), lambda i, h, a, b: ((b[layers + 1 - int(keep)] * strips + i) * 2 + h, 0))
        ]
        + [pl.BlockSpec(x.shape, lambda i, h, a, b: (0, 0)) for x in pieces],
        out_specs=pl.BlockSpec((layers, 1, width, wide), lambda i, h, a, b: (0, i, 0, 0)),
        scratch_shapes=[pltpu.VMEM((depth, wide), BF)],
    )
    out = pl.pallas_call(
        functools.partial(first_kernel, keep),
        out_shape=jax.ShapeDtypeStruct((layers, strips, width, wide), F32),
        grid_spec=grid_spec,
        cost_estimate=pl.CostEstimate(
            flops=tile_rows * depth * wide,
            bytes_accessed=tile_rows * depth + 2 * tile_rows * wide,
            transcendentals=0,
        ),
        name="first",
    )(spots, chips, amplitudes, *pieces)
    return out.reshape(layers * strips * width, wide)


def second_kernel(groups, layers, place, chips, *refs):
    lhs = refs[:groups]
    rhs = refs[groups : groups + layers]
    gap_rows, gap_cols = refs[groups + layers], refs[groups + layers + 1]
    out_ref, left, right = refs[-3], refs[-2], refs[-1]
    dims = (((1,), (1,)), ((), ()))
    width = rhs[0].shape[0]

    @pl.when(pl.program_id(0) == 0)
    def _():
        for n in range(layers):
            right[pl.ds(pl.multiple_of(chips[n] * width, 32), width), :] = rhs[n][...]

    start = 0
    for part in lhs:
        wide = part.shape[3]
        for n in range(layers):
            left[n * width : (n + 1) * width, start : start + wide] = part[chips[n], 0]
        start += wide
    broad = out_ref.shape[1]
    pick = 512 if broad % 512 == 0 else broad
    rows = jnp.transpose(jnp.broadcast_to(gap_rows[...], (LANES, gap_rows.shape[1])))[:, :1]
    for n in range(0, broad, pick):
        total = lax.dot_general(
            left[...], right[n : n + pick, :], dims, preferred_element_type=jnp.float32
        )
        out_ref[:, n : n + pick] = (-total / (rows + gap_cols[:, n : n + pick])).astype(out_ref.dtype)


def second_product(lhs, rhs, gap_rows, gap_cols, place, chips, strips, out, shape):
    layers = len(rhs)
    width, naux = rhs[0].shape
    tall = layers * width
    lhs = [x.reshape(layers, strips, width, x.shape[1]) for x in lhs]
    in_specs = [pl.BlockSpec((layers, 1, width, x.shape[3]), lambda i, a, b: (0, i, 0, 0)) for x in lhs]
    in_specs += [pl.BlockSpec((width, naux), lambda i, a, b: (0, 0)) for x in rhs]
    in_specs += [
        pl.BlockSpec((1, tall), lambda i, a, b: (0, a[0] * strips + i)),
        pl.BlockSpec((1, tall), lambda i, a, b: (0, a[1])),
    ]
    operands = [*lhs, *rhs, gap_rows, gap_cols]
    aliases = {}
    if out is not None:
        in_specs.append(pl.BlockSpec(memory_space=pl.ANY))
        aliases = {2 + len(operands): 0}
        operands.append(out)
    grid_spec = pltpu.PrefetchScalarGridSpec(
        num_scalar_prefetch=2,
        grid=(strips,),
        in_specs=in_specs,
        out_specs=pl.BlockSpec((tall, tall), lambda i, a, b: (a[0] * strips + i, a[1])),
        scratch_shapes=[pltpu.VMEM((tall, naux), BF), pltpu.VMEM((tall, naux), BF)],
    )
    return pl.pallas_call(
        functools.partial(second_kernel, len(lhs), layers),
        out_shape=jax.ShapeDtypeStruct(shape, BF),
        grid_spec=grid_spec,
        input_output_aliases=aliases,
        cost_estimate=pl.CostEstimate(
            flops=2 * strips * tall * tall * naux,
            bytes_accessed=2 * strips * tall * (naux + tall),
            transcendentals=0,
        ),
        name="second",
    )(place, chips, *operands)


def body(layers, amplitudes, cholesky, occ_map, vir_map):
    tile_rows, tile_cols = amplitudes.shape
    piece, naux = cholesky.shape
    row = lax.axis_index("row")
    c = lax.axis_index("col")
    k, j = row // 2, row % 2
    mid = piece // 2
    strips = 3 if piece % 768 == 0 else 1
    width = piece // strips
    cut = (2 * naux // 5) // 256 * 256
    spans = [(0, cut), (cut, naux)] if cut else [(0, naux)]
    chunks = len(spans)

    def line(x):
        ups, downs = [x], [x]
        for s in range(1, layers):
            up = [(n, n + 1) for n in range(s - 1, layers - 1)]
            down = [(layers - 1 - a, layers - 1 - b) for a, b in up]
            ups.append(lax.ppermute(ups[-1], "col", up))
            downs.append(lax.ppermute(downs[-1], "col", down))
        return ups[:0:-1] + [x] + downs[1:]

    def across(x, d):
        return lax.ppermute(x, "row", [(n, n ^ (2 * d)) for n in range(2 * layers)])

    def swap(x):
        return lax.ppermute(x, "row", [(n, n ^ 1) for n in range(2 * layers)])

    reach = jnp.arange(1 - layers, layers, dtype=jnp.int32) + c
    chips = jnp.bitwise_xor(k, jnp.arange(layers, dtype=jnp.int32))
    sides = jnp.concatenate([chips, jnp.stack([j, 1 - j])]).astype(jnp.int32)
    spots = jnp.where(jnp.logical_and(reach >= 0, reach < layers), reach * piece, -1)
    spots = jnp.concatenate([spots, (k == c).astype(jnp.int32)[None]]).astype(jnp.int32)

    gap_rows = pair_gap(
        lax.dynamic_slice_in_dim(occ_map, c * tile_rows, tile_rows, 0),
        lax.dynamic_slice_in_dim(vir_map, c * tile_rows, tile_rows, 0),
    )[None, :]
    gap_cols = pair_gap(
        lax.dynamic_slice_in_dim(occ_map, row * tile_cols, tile_cols, 0),
        lax.dynamic_slice_in_dim(vir_map, row * tile_cols, tile_cols, 0),
    )[None, :]

    shares = []
    for lo, hi in spans:
        pieces = line(cholesky[:, lo:hi])
        sent = first_product(amplitudes, pieces, spots, sides, layers, strips, False)
        kept = first_product(amplitudes, pieces, spots, sides, layers, strips, True)
        came = swap(sent)

        def both(d, part=None, kept=kept, came=came):
            at = slice(d * piece, (d + 1) * piece)
            if part is not None:
                at = slice(d * piece + part * mid, d * piece + (part + 1) * mid)
            return kept[at] + came[at]

        if layers == 4:
            a0 = jnp.concatenate([both(1, 0), both(3, 0)]).astype(BF)
            b0 = jnp.concatenate([both(2, 1), both(3, 1)]).astype(BF)
            a1, b1 = across(a0, 1), across(b0, 2)
            kept, came, a1, b1 = lax.optimization_barrier((kept, came, a1, b1))
            a2 = (both(2, 0, kept, came) + a1[mid:].astype(F32)).astype(BF)
            b2 = (both(1, 1, kept, came) + b1[mid:].astype(F32)).astype(BF)
            a2, b2 = across(a2, 2), across(b2, 1)
            kept, came, a1, b1, a2, b2 = lax.optimization_barrier((kept, came, a1, b1, a2, b2))
            top = both(0, 0, kept, came) + a1[:mid].astype(F32) + a2.astype(F32)
            low = both(0, 1, kept, came) + b1[:mid].astype(F32) + b2.astype(F32)
            total = jnp.concatenate([top, low])
        else:
            total = both(0)
            for d in range(1, layers):
                total = total + across(both(d).astype(BF), d).astype(F32)
        shares.append(total.astype(BF))

    splits = [(0, chunks - 1), (chunks - 1, chunks)] if chunks > 1 else [(0, 1)]
    near, far = [], []
    for lo, hi in splits:
        mine = jnp.concatenate(shares[lo:hi], axis=1)
        if layers == 4:
            a, b = across(mine, 1), across(mine, 2)
            parts = [mine, a, b, across(a[:mid], 2), across(b[mid:], 1)]
        else:
            parts = [mine] + [across(mine, d) for d in range(1, layers)]
        near.append(jnp.concatenate(parts, axis=0))
        far.append(swap(near[-1]))

    early = [line(x) for x in shares[:-1]]
    near_at = lambda s: jnp.stack([j, jnp.full_like(j, s)]).astype(jnp.int32)
    far_at = lambda s: jnp.stack([1 - j, jnp.full_like(j, s)]).astype(jnp.int32)
    out = None
    for s in range(strips):
        at = slice(s * width, (s + 1) * width)
        late = line(shares[-1][at])
        ahead, late = lax.optimization_barrier((early, late))
        rows = [[x[at] for x in group] for group in ahead] + [late]

        def block(d, rows=rows):
            owner = jnp.bitwise_xor(k, d) - c + layers - 1
            return jnp.concatenate([lax.select_n(owner, *group) for group in rows], axis=1)

        blocks = [block(d) for d in range(layers)]
        pair = jnp.concatenate([blocks[1], blocks[-1]])
        if layers == 4:
            one = across(pair, 1)
            two = across(blocks[2], 2)
            rest = one[width:]
            rhs = [blocks[0], one, two, across(rest, 2)]
        else:
            rhs = [blocks[0]] + [across(blocks[d], d) for d in range(1, layers)]
        shape = (tile_rows, tile_cols)
        out = second_product(near, rhs, gap_rows, gap_cols, near_at(s), sides, strips, out, shape)
        out = second_product(far, rhs, gap_rows, gap_cols, far_at(s), sides, strips, out, shape)
    return out


def solution(mesh):
    layers = mesh.shape["col"]
    assert mesh.shape["row"] == 2 * layers

    def run(*args):
        return body(layers, *args)

    return jax.shard_map(
        run,
        mesh=mesh,
        in_specs=(P("col", "row"), P(("row", "col"), None), P(), P()),
        out_specs=P("col", "row"),
        check_vma=False,
    )
```

time: 886 us -> 614 us (0.69)
  waiting for transfers between devices: 694 us -> 298 us
  Pallas kernels: 0 us -> 165 us
  matrix products: 115 us -> 0 us
  starting transfers between devices: 0.3 us -> 87.3 us
  local copies, waits for them, and re-layouts: 36.3 us -> 16.8 us
  other arithmetic: 25.5 us -> 43.1 us
  between operations: 13.2 us -> 1.1 us
    ppermute x0 -> x65, waiting for transfers between devices: none -> 298 us  [the longest x25 152 us: across(): return lax.ppermute(x, 'row', [(n, n ^ 2 * d) for n in range(2 * layers)])]
    psum x1 -> x0, waiting for transfers between devices: 272 us -> none  [broadcast(): return lax.psum(jnp.where(mine, x, jnp.zeros_like(x)), axis)]
    all_gather x2 -> x0, waiting for transfers between devices: 231 us -> none  [the longest x1 145 us: body(): piece = lax.all_gather(cholesky, 'col', axis=0, tiled=True)]
    reduce_scatter x1 -> x0, waiting for transfers between devices: 190 us -> none  [body(): lax.psum_scatter(partial_value, 'row', scatter_dimension=0, tiled=True)]
    pallas_call x0 -> x10, Pallas kernels: none -> 165 us  [the longest x4 83.6 us: first_product(): pl.pallas_call(functools.partial(first_kernel, keep), out_shape=jax.Shape...]
    dot_general x2 -> x0, matrix products: 115 us -> none  [the longest x1 58.6 us: body(): total = jnp.dot(amplitudes, piece, preferred_element_type=jnp.float32)]
    ppermute x0 -> x65, starting transfers between devices: none -> 87.3 us  [the longest x18 35.8 us: line(): ups.append(lax.ppermute(ups[-1], 'col', up))]
    dynamic_update_slice x1 -> x0, local copies, waits for them, and re-layouts: 36.3 us -> none  [body(): lax.dynamic_update_slice_in_dim(total, current + on_diag * piece.astype(j...]
  transfers between devices with their start and end apart: 4 -> 65, of which waited for: 4 -> 30; matrix products, arithmetic and copies ran while one was open for 0% -> 8% of each run, Pallas kernels for 0% -> 23%
where the time goes in v1:
time: 614 us; the launch traced here: 612 us
  waiting for transfers between devices  298 us (49%)
  Pallas kernels  165 us (27%)
  starting transfers between devices  87.3 us (14%)
  other arithmetic  43.1 us (7%)
  local copies, waits for them, and re-layouts  16.8 us (3%)
    ppermute x25, waiting for transfers between devices, across(): return lax.ppermute(x, 'row', [(n, n ^ 2 * d) for n in range(2 * layers)])  152 us
    ppermute x18, waiting for transfers between devices, line(): downs.append(lax.ppermute(downs[-1], 'col', down))  99.9 us
    pallas_call x4, Pallas kernels, first_product(): pl.pallas_call(functools.partial(first_kernel, keep), out_shape=jax.Shape...  83.6 us
    pallas_call x6, Pallas kernels, second_product(): pl.pallas_call(functools.partial(second_kernel, len(lhs), layers), out_sh...  81.7 us
    ppermute x18, waiting for transfers between devices, line(): ups.append(lax.ppermute(ups[-1], 'col', up))  46 us
    ppermute x18, starting transfers between devices, line(): ups.append(lax.ppermute(ups[-1], 'col', up))  35.8 us
    ppermute x25, starting transfers between devices, across(): return lax.ppermute(x, 'row', [(n, n ^ 2 * d) for n in range(2 * layers)])  28 us
    ppermute x18, starting transfers between devices, line(): downs.append(lax.ppermute(downs[-1], 'col', down))  23.3 us
  transfers between devices with their start and end apart: 65, of which 30 were waited for; matrix products, arithmetic and copies ran while one was open for 8% of the time, Pallas kernels for 23%

profile of v1, /device:TPU:0, one launch (start us, length us, event | category | flops | bytes accessed | tf_op | source)
XLA Modules:
  0.0 611.9 jit_solution(2462744595515803416)
XLA Ops:
  14.8 33.6 %collective-permute-done.refs_2_ = bf16[768,512]{1,0:T(8,128)(2,1)S(1)} collective-permute-done((bf16[768,512]{1,0:T(8,128)(2,1)S(1)}, bf16[768,512]{1,0:T(8,128)(2,1)S(1)}, u32[]{:S(2)}, u32[]{:S(2)}) %collective-permute-start) | collective-permute-done | bytes 786464 | tf_op jit(solution)/shard_map/ppermute | solution.py:163
  58.4 17.2 %collective-permute-done.4.refs_5_ = bf16[768,512]{1,0:T(8,128)(2,1)} collective-permute-done((bf16[768,512]{1,0:T(8,128)(2,1)S(1)}, bf16[768,512]{1,0:T(8,128)(2,1)}, u32[]{:S(2)}, u32[]{:S(2)}) %collective-permute-start.4) | collective-permute-done | bytes 786464 | tf_op jit(solution)/shard_map/ppermute | solution.py:164
  78.7 22.2 %collective-permute-done.20.refs_5_ = bf16[768,768]{1,0:T(8,128)(2,1)} collective-permute-done((bf16[768,768]{1,0:T(8,128)(2,1)}, bf16[768,768]{1,0:T(8,128)(2,1)}, u32[]{:S(2)}, u32[]{:S(2)}) %collective-permute-start.20) | collective-permute-done | bytes 1179680 | tf_op jit(solution)/shard_map/ppermute | solution.py:164
  103.5 14.3 %collective-permute-done.5.refs_6_ = bf16[768,512]{1,0:T(8,128)(2,1)} collective-permute-done((bf16[768,512]{1,0:T(8,128)(2,1)}, bf16[768,512]{1,0:T(8,128)(2,1)}, u32[]{:S(2)}, u32[]{:S(2)}) %collective-permute-start.5) | collective-permute-done | bytes 786464 | tf_op jit(solution)/shard_map/ppermute | solution.py:164
  117.8 18.2 %first.5 = f32[4,3,256,512]{3,2,1,0:T(8,128)} custom-call(s32[8]{0:T(128)} %pad_add_fusion.7.spots, s32[6]{0:T(128)} %pad_add_fusion.6.chips, bf16[6144,3072]{1,0:T(8,128)(2,1)} %t_ref.7, bf16[768,512]{1,0:T(8,128)(2,1)} %collective-permute-done.2.refs_0_, bf16[768,512]{1,0:T(8,128)(2,1)} %collective-permute-done.1.refs_1_, bf16[768,512]{1,0:T(8,128)(2,1)} %copy-done.29, ...), custom_call_target="tpu_custom_call" | custom-call | flops 9663676416 | bytes 25165824 | tf_op jit(solution)/shard_map/first/pallas_call | solution.py:64
  141.1 23.5 %first.7 = f32[4,3,256,768]{3,2,1,0:T(8,128)} custom-call(s32[8]{0:T(128)} %pad_add_fusion.7.spots, s32[6]{0:T(128)} %pad_add_fusion.6.chips, bf16[6144,3072]{1,0:T(8,128)(2,1)} %t_ref.7, bf16[768,768]{1,0:T(8,128)(2,1)} %collective-permute-done.18.refs_0_, bf16[768,768]{1,0:T(8,128)(2,1)} %collective-permute-done.17.refs_1_, bf16[768,768]{1,0:T(8,128)(2,1)} %copy-done.24, ...), custom_call_target="tpu_custom_call" | custom-call | flops 14495514624 | bytes 28311552 | tf_op jit(solution)/shard_map/first/pallas_call | solution.py:64
  164.6 18.3 %first.4 = f32[4,3,256,512]{3,2,1,0:T(8,128)} custom-call(s32[8]{0:T(128)} %pad_add_fusion.7.spots, s32[6]{0:T(128)} %pad_add_fusion.6.chips, bf16[6144,3072]{1,0:T(8,128)(2,1)} %t_ref.7, bf16[768,512]{1,0:T(8,128)(2,1)} %collective-permute-done.2.refs_0_, bf16[768,512]{1,0:T(8,128)(2,1)} %collective-permute-done.1.refs_1_, bf16[768,512]{1,0:T(8,128)(2,1)} %copy-done.29, ...), custom_call_target="tpu_custom_call" | custom-call | flops 9663676416 | bytes 25165824 | tf_op jit(solution)/shard_map/first/pallas_call | solution.py:64
  189.5 16.8 %collective-permute-done.8 = bf16[768,512]{1,0:T(8,128)(2,1)S(1)} collective-permute-done((bf16[768,512]{1,0:T(8,128)(2,1)S(1)}, bf16[768,512]{1,0:T(8,128)(2,1)S(1)}, u32[]{:S(2)}, u32[]{:S(2)}) %collective-permute-start.8) | collective-permute-done | bytes 786464 | tf_op jit(solution)/shard_map/ppermute | solution.py:168
  212.3 23.5 %first.6 = f32[4,3,256,768]{3,2,1,0:T(8,128)} custom-call(s32[8]{0:T(128)} %pad_add_fusion.7.spots, s32[6]{0:T(128)} %pad_add_fusion.6.chips, bf16[6144,3072]{1,0:T(8,128)(2,1)} %t_ref.7, bf16[768,768]{1,0:T(8,128)(2,1)} %collective-permute-done.18.refs_0_, bf16[768,768]{1,0:T(8,128)(2,1)} %collective-permute-done.17.refs_1_, bf16[768,768]{1,0:T(8,128)(2,1)} %copy-done.24, ...), custom_call_target="tpu_custom_call" | custom-call | flops 14495514624 | bytes 28311552 | tf_op jit(solution)/shard_map/first/pallas_call | solution.py:64
  250.7 12.4 %collective-permute-done.32 = bf16[768,512]{1,0:T(8,128)(2,1)S(1)} collective-permute-done((bf16[768,512]{1,0:T(8,128)(2,1)S(1)}, bf16[768,512]{1,0:T(8,128)(2,1)S(1)}, u32[]{:S(2)}, u32[]{:S(2)}) %collective-permute-start.32) | collective-permute-done | bytes 786464 | tf_op jit(solution)/shard_map/ppermute | solution.py:163
  276.5 10.8 %collective-permute-done.11 = bf16[768,512]{1,0:T(8,128)(2,1)S(1)} collective-permute-done((bf16[768,512]{1,0:T(8,128)(2,1)S(1)}, bf16[768,512]{1,0:T(8,128)(2,1)S(1)}, u32[]{:S(2)}, u32[]{:S(2)}) %collective-permute-start.11) | collective-permute-done | bytes 786464 | tf_op jit(solution)/shard_map/ppermute | solution.py:168
  291.0 9.7 %collective-permute-done.25 = bf16[384,768]{1,0:T(8,128)(2,1)S(1)} collective-permute-done((bf16[384,768]{1,0:T(8,128)(2,1)S(1)}, bf16[384,768]{1,0:T(8,128)(2,1)S(1)}, u32[]{:S(2)}, u32[]{:S(2)}) %collective-permute-start.25) | collective-permute-done | bytes 589856 | tf_op jit(solution)/shard_map/ppermute | solution.py:168
  369.8 11.7 %collective-permute-done.61 = bf16[256,768]{1,0:T(8,128)(2,1)S(1)} collective-permute-done((bf16[256,768]{1,0:T(8,128)(2,1)}, bf16[256,768]{1,0:T(8,128)(2,1)S(1)}, u32[]{:S(2)}, u32[]{:S(2)}) %collective-permute-start.61) | collective-permute-done | bytes 393248 | tf_op jit(solution)/shard_map/ppermute | solution.py:164
  387.5 13.1 %collective-permute-done.27 = bf16[768,768]{1,0:T(8,128)(2,1)S(1)} collective-permute-done((bf16[768,768]{1,0:T(8,128)(2,1)S(1)}, bf16[768,768]{1,0:T(8,128)(2,1)S(1)}, u32[]{:S(2)}, u32[]{:S(2)}) %collective-permute-start.27) | collective-permute-done | bytes 1179680 | tf_op jit(solution)/shard_map/ppermute | solution.py:168
  435.2 20.6 %collective-permute-done.62.refs_3_ = bf16[512,1280]{1,0:T(8,128)(2,1)S(1)} collective-permute-done((bf16[512,1280]{1,0:T(8,128)(2,1)S(1)}, bf16[512,1280]{1,0:T(8,128)(2,1)S(1)}, u32[]{:S(2)}, u32[]{:S(2)}) %collective-permute-start.62) | collective-permute-done | bytes 1310752 | tf_op jit(solution)/shard_map/ppermute | solution.py:168
  456.9 27.0 %collective-permute-done.53.refs_3_ = bf16[512,1280]{1,0:T(8,128)(2,1)S(1)} collective-permute-done((bf16[512,1280]{1,0:T(8,128)(2,1)S(1)}, bf16[512,1280]{1,0:T(8,128)(2,1)S(1)}, u32[]{:S(2)}, u32[]{:S(2)}) %collective-permute-start.53) | collective-permute-done | bytes 1310752 | tf_op jit(solution)/shard_map/ppermute | solution.py:168
  487.8 22.9 %collective-permute-done.44.refs_3_ = bf16[512,1280]{1,0:T(8,128)(2,1)S(1)} collective-permute-done((bf16[512,1280]{1,0:T(8,128)(2,1)S(1)}, bf16[512,1280]{1,0:T(8,128)(2,1)S(1)}, u32[]{:S(2)}, u32[]{:S(2)}) %collective-permute-start.44) | collective-permute-done | bytes 1310752 | tf_op jit(solution)/shard_map/ppermute | solution.py:168
  514.7 13.8 %second.6.refs_8_ = bf16[6144,3072]{1,0:T(8,128)(2,1)} custom-call(s32[2]{0:T(128)} %pad_add_fusion.4.place, s32[6]{0:T(128)} %pad_add_fusion.6.chips, bf16[4,3,256,512]{3,2,1,0:T(8,128)(2,1)} %bitcast.19, bf16[4,3,256,768]{3,2,1,0:T(8,128)(2,1)} %bitcast.12.refs_1_, bf16[256,1280]{1,0:T(8,128)(2,1)} %pad_maximum_fusion.10.refs_2_, ...), custom_call_target="tpu_custom_call" | custom-call | flops 8053063680 | bytes 14155776 | tf_op jit(solution)/shard_map/second/pallas_call | solution.py:131
  529.6 13.6 %second.7.refs_8_ = bf16[6144,3072]{1,0:T(8,128)(2,1)} custom-call(s32[2]{0:T(128)} %pad_add_fusion.5.place, s32[6]{0:T(128)} %pad_add_fusion.6.chips, bf16[4,3,256,512]{3,2,1,0:T(8,128)(2,1)} %bitcast.5.refs_0_, bf16[4,3,256,768]{3,2,1,0:T(8,128)(2,1)} %bitcast.8.refs_1_, ...), custom_call_target="tpu_custom_call", output_to_operand_aliasing={{}: (10, {})} | custom-call | flops 8053063680 | bytes 14155776 | tf_op jit(solution)/shard_map/second/pallas_call | solution.py:131
  543.2 13.5 %collective-permute-done.55.refs_5_ = bf16[256,1280]{1,0:T(8,128)(2,1)} collective-permute-done((bf16[256,1280]{1,0:T(8,128)(2,1)}, bf16[256,1280]{1,0:T(8,128)(2,1)}, u32[]{:S(2)}, u32[]{:S(2)}) %collective-permute-start.55) | collective-permute-done | bytes 655392 | tf_op jit(solution)/shard_map/ppermute | solution.py:168
  556.7 13.6 %second.8.refs_8_ = bf16[6144,3072]{1,0:T(8,128)(2,1)} custom-call(s32[2]{0:T(128)} %pad_add_fusion.2.place, s32[6]{0:T(128)} %pad_add_fusion.6.chips, bf16[4,3,256,512]{3,2,1,0:T(8,128)(2,1)} %bitcast.20, bf16[4,3,256,768]{3,2,1,0:T(8,128)(2,1)} %bitcast.12.refs_1_, bf16[256,1280]{1,0:T(8,128)(2,1)} %pad_maximum_fusion.8.refs_2_, ...), custom_call_target="tpu_custom_call", output_to_operand_aliasing={{}: (10, {})} | custom-call | flops 8053063680 | bytes 14155776 | tf_op jit(solution)/shard_map/second/pallas_call | solution.py:131
  570.3 13.6 %second.9.refs_8_ = bf16[6144,3072]{1,0:T(8,128)(2,1)} custom-call(s32[2]{0:T(128)} %pad_add_fusion.3.place, s32[6]{0:T(128)} %pad_add_fusion.6.chips, bf16[4,3,256,512]{3,2,1,0:T(8,128)(2,1)} %bitcast.5.refs_0_, bf16[4,3,256,768]{3,2,1,0:T(8,128)(2,1)} %bitcast.8.refs_1_, ...), custom_call_target="tpu_custom_call", output_to_operand_aliasing={{}: (10, {})} | custom-call | flops 8053063680 | bytes 14155776 | tf_op jit(solution)/shard_map/second/pallas_call | solution.py:131
  584.7 13.6 %second.10.refs_8_ = bf16[6144,3072]{1,0:T(8,128)(2,1)} custom-call(s32[2]{0:T(128)} %get-tuple-element.164.place, s32[6]{0:T(128)} %pad_add_fusion.6.chips, bf16[4,3,256,512]{3,2,1,0:T(8,128)(2,1)} %bitcast.21, bf16[4,3,256,768]{3,2,1,0:T(8,128)(2,1)} %bitcast.12.refs_1_, ...), custom_call_target="tpu_custom_call", output_to_operand_aliasing={{}: (10, {})} | custom-call | flops 8053063680 | bytes 14155776 | tf_op jit(solution)/shard_map/second/pallas_call | solution.py:131
  598.3 13.6 %second.11 = bf16[6144,3072]{1,0:T(8,128)(2,1)} custom-call(s32[2]{0:T(128)} %get-tuple-element.165.place, s32[6]{0:T(128)} %pad_add_fusion.6.chips, bf16[4,3,256,512]{3,2,1,0:T(8,128)(2,1)} %bitcast.5.refs_0_, bf16[4,3,256,768]{3,2,1,0:T(8,128)(2,1)} %bitcast.8.refs_1_, ...), custom_call_target="tpu_custom_call", output_to_operand_aliasing={{}: (10, {})} | custom-call | flops 8053063680 | bytes 14155776 | tf_op jit(solution)/shard_map/second/pallas_call | solution.py:131
  (279 shorter events, 199.8 us)
Async XLA Ops:
  1.4 52.5 %collective-permute-start.16 = (bf16[768,768]{1,0:T(8,128)(2,1)S(1)}, bf16[768,768]{1,0:T(8,128)(2,1)S(1)}, u32[]{:S(2)}, u32[]{:S(2)}) collective-permute-start(bf16[768,768]{1,0:T(8,128)(2,1)S(1)} %slice.244.refs_3_), channel_id=1, source_target_pairs={{0,1},{1,2},{2,3},{4,5},{5,6},{6,7},{8,9},{9,10},{10,11},{12,13},{... | collective-permute-start | bytes 3538952 | tf_op jit(solution)/shard_map/ppermute | solution.py:163
  6.4 49.2 %collective-permute-start.19 = (bf16[768,768]{1,0:T(8,128)(2,1)S(1)}, bf16[768,768]{1,0:T(8,128)(2,1)}, u32[]{:S(2)}, u32[]{:S(2)}) collective-permute-start(bf16[768,768]{1,0:T(8,128)(2,1)S(1)} %slice.244.refs_3_), channel_id=1, source_target_pairs={{3,2},{2,1},{1,0},{7,6},{6,5},{5,4},{11,10},{10,9},{9,8},{15,14},{... | collective-permute-start | bytes 3538952 | tf_op jit(solution)/shard_map/ppermute | solution.py:164
  8.9 39.5 %collective-permute-start = (bf16[768,512]{1,0:T(8,128)(2,1)S(1)}, bf16[768,512]{1,0:T(8,128)(2,1)S(1)}, u32[]{:S(2)}, u32[]{:S(2)}) collective-permute-start(bf16[768,512]{1,0:T(8,128)(2,1)S(1)} %slice.221.refs_3_), channel_id=1, source_target_pairs={{0,1},{1,2},{2,3},{4,5},{5,6},{6,7},{8,9},{9,10},{10,11},{12,13},{... | collective-permute-start | bytes 2359304 | tf_op jit(solution)/shard_map/ppermute | solution.py:163
  13.5 39.1 %collective-permute-start.3 = (bf16[768,512]{1,0:T(8,128)(2,1)S(1)}, bf16[768,512]{1,0:T(8,128)(2,1)S(1)}, u32[]{:S(2)}, u32[]{:S(2)}) collective-permute-start(bf16[768,512]{1,0:T(8,128)(2,1)S(1)} %slice.221.refs_3_), channel_id=1, source_target_pairs={{3,2},{2,1},{1,0},{7,6},{6,5},{5,4},{11,10},{10,9},{9,8},{15,14},{... | collective-permute-start | bytes 2359304 | tf_op jit(solution)/shard_map/ppermute | solution.py:164
  55.6 45.4 %collective-permute-start.20 = (bf16[768,768]{1,0:T(8,128)(2,1)}, bf16[768,768]{1,0:T(8,128)(2,1)}, u32[]{:S(2)}, u32[]{:S(2)}) collective-permute-start(bf16[768,768]{1,0:T(8,128)(2,1)} %collective-permute-done.19.refs_4_), channel_id=1, source_target_pairs={{2,1},{1,0},{6,5},{5,4},{10,9},{9,8},{14,13},{13,12},{18,17},{17,1... | collective-permute-start | bytes 3538952 | tf_op jit(solution)/shard_map/ppermute | solution.py:164
  56.9 46.6 %collective-permute-start.2 = (bf16[768,512]{1,0:T(8,128)(2,1)}, bf16[768,512]{1,0:T(8,128)(2,1)}, u32[]{:S(2)}, u32[]{:S(2)}) collective-permute-start(bf16[768,512]{1,0:T(8,128)(2,1)} %collective-permute-done.1.refs_1_), channel_id=1, source_target_pairs={{2,3},{6,7},{10,11},{14,15},{18,19},{22,23},{26,27},{30,31}} | collective-permute-start | bytes 2359304 | tf_op jit(solution)/shard_map/ppermute | solution.py:163
  75.7 42.1 %collective-permute-start.5 = (bf16[768,512]{1,0:T(8,128)(2,1)}, bf16[768,512]{1,0:T(8,128)(2,1)}, u32[]{:S(2)}, u32[]{:S(2)}) collective-permute-start(bf16[768,512]{1,0:T(8,128)(2,1)} %collective-permute-done.4.refs_5_), channel_id=1, source_target_pairs={{1,0},{5,4},{9,8},{13,12},{17,16},{21,20},{25,24},{29,28}} | collective-permute-start | bytes 2359304 | tf_op jit(solution)/shard_map/ppermute | solution.py:164
  77.0 59.1 %collective-permute-start.18 = (bf16[768,768]{1,0:T(8,128)(2,1)}, bf16[768,768]{1,0:T(8,128)(2,1)}, u32[]{:S(2)}, u32[]{:S(2)}) collective-permute-start(bf16[768,768]{1,0:T(8,128)(2,1)} %collective-permute-done.17.refs_1_), channel_id=1, source_target_pairs={{2,3},{6,7},{10,11},{14,15},{18,19},{22,23},{26,27},{30,31}} | collective-permute-start | bytes 3538952 | tf_op jit(solution)/shard_map/ppermute | solution.py:163
  100.9 40.1 %collective-permute-start.21 = (bf16[768,768]{1,0:T(8,128)(2,1)}, bf16[768,768]{1,0:T(8,128)(2,1)}, u32[]{:S(2)}, u32[]{:S(2)}) collective-permute-start(bf16[768,768]{1,0:T(8,128)(2,1)} %collective-permute-done.20.refs_5_), channel_id=1, source_target_pairs={{1,0},{5,4},{9,8},{13,12},{17,16},{21,20},{25,24},{29,28}} | collective-permute-start | bytes 3538952 | tf_op jit(solution)/shard_map/ppermute | solution.py:164
  136.0 46.9 %collective-permute-start.6 = (f32[3072,512]{1,0:T(8,128)}, f32[3072,512]{1,0:T(8,128)}, u32[]{:S(2)}, u32[]{:S(2)}) collective-permute-start(f32[3072,512]{1,0:T(8,128)} %bitcast.27), channel_id=1, source_target_pairs={{0,4},{4,0},{8,12},{12,8},{16,20},{20,16},{24,28},{28,24},{1,5},{5... | collective-permute-start | bytes 18874376 | tf_op jit(solution)/shard_map/ppermute | solution.py:171
  164.6 73.2 %collective-permute-start.22 = (f32[3072,768]{1,0:T(8,128)}, f32[3072,768]{1,0:T(8,128)}, u32[]{:S(2)}, u32[]{:S(2)}) collective-permute-start(f32[3072,768]{1,0:T(8,128)} %bitcast.26), channel_id=1, source_target_pairs={{0,4},{4,0},{8,12},{12,8},{16,20},{20,16},{24,28},{28,24},{1,5},{5... | collective-permute-start | bytes 28311560 | tf_op jit(solution)/shard_map/ppermute | solution.py:171
  249.1 38.2 %collective-permute-start.11 = (bf16[768,512]{1,0:T(8,128)(2,1)S(1)}, bf16[768,512]{1,0:T(8,128)(2,1)S(1)}, u32[]{:S(2)}, u32[]{:S(2)}) collective-permute-start(bf16[768,512]{1,0:T(8,128)(2,1)S(1)} %pad_maximum_fusion.5), channel_id=1, source_target_pairs={{0,8},{4,12},{8,0},{12,4},{16,24},{20,28},{24,16},{28,20},{1,9},{5... | collective-permute-start | bytes 2359304 | tf_op jit(solution)/shard_map/ppermute | solution.py:168
  348.8 34.3 %collective-permute-start.39 = (bf16[256,768]{1,0:T(8,128)(2,1)S(1)}, bf16[256,768]{1,0:T(8,128)(2,1)S(1)}, u32[]{:S(2)}, u32[]{:S(2)}) collective-permute-start(bf16[256,768]{1,0:T(8,128)(2,1)S(1)} %copy-done.35), channel_id=1, source_target_pairs={{1,2},{2,3},{5,6},{6,7},{9,10},{10,11},{13,14},{14,15},{17,18},{18... | collective-permute-start | bytes 1179656 | tf_op jit(solution)/shard_map/ppermute | solution.py:163
  383.1 145.5 %collective-permute-start.15 = (bf16[3072,512]{1,0:T(8,128)(2,1)S(1)}, bf16[3072,512]{1,0:T(8,128)(2,1)}, u32[]{:S(2)}, u32[]{:S(2)}) collective-permute-start(bf16[3072,512]{1,0:T(8,128)(2,1)S(1)} %constant_dynamic-update-slice_fusion), channel_id=1, source_target_pairs={{0,4},{4,0},{8,12},{12,8},{16,20},{20,16},{24,28},{28,24},{1,5},{5... | collective-permute-start | bytes 9437192 | tf_op jit(solution)/shard_map/ppermute | solution.py:171
  384.3 43.2 %collective-permute-start.40 = (bf16[256,768]{1,0:T(8,128)(2,1)S(1)}, bf16[256,768]{1,0:T(8,128)(2,1)S(1)}, u32[]{:S(2)}, u32[]{:S(2)}) collective-permute-start(bf16[256,768]{1,0:T(8,128)(2,1)S(1)} %collective-permute-done.39), channel_id=1, source_target_pairs={{2,3},{6,7},{10,11},{14,15},{18,19},{22,23},{26,27},{30,31}} | collective-permute-start | bytes 1179656 | tf_op jit(solution)/shard_map/ppermute | solution.py:163
  385.7 43.4 %collective-permute-start.43 = (bf16[256,768]{1,0:T(8,128)(2,1)S(1)}, bf16[256,768]{1,0:T(8,128)(2,1)S(1)}, u32[]{:S(2)}, u32[]{:S(2)}) collective-permute-start(bf16[256,768]{1,0:T(8,128)(2,1)S(1)} %collective-permute-done.42), channel_id=1, source_target_pairs={{1,0},{5,4},{9,8},{13,12},{17,16},{21,20},{25,24},{29,28}} | collective-permute-start | bytes 1179656 | tf_op jit(solution)/shard_map/ppermute | solution.py:164
  427.4 102.2 %collective-permute-start.31 = (bf16[3072,768]{1,0:T(8,128)(2,1)}, bf16[3072,768]{1,0:T(8,128)(2,1)}, u32[]{:S(2)}, u32[]{:S(2)}) collective-permute-start(bf16[3072,768]{1,0:T(8,128)(2,1)} %constant_dynamic-update-slice_fusion.6), channel_id=1, source_target_pairs={{0,4},{4,0},{8,12},{12,8},{16,20},{20,16},{24,28},{28,24},{1,5},{5... | collective-permute-start | bytes 14155784 | tf_op jit(solution)/shard_map/ppermute | solution.py:171
  427.5 56.4 %collective-permute-start.53 = (bf16[512,1280]{1,0:T(8,128)(2,1)S(1)}, bf16[512,1280]{1,0:T(8,128)(2,1)S(1)}, u32[]{:S(2)}, u32[]{:S(2)}) collective-permute-start(bf16[512,1280]{1,0:T(8,128)(2,1)S(1)} %maximum_maximum_fusion.1), channel_id=1, source_target_pairs={{0,8},{4,12},{8,0},{12,4},{16,24},{20,28},{24,16},{28,20},{1,9},{5... | collective-permute-start | bytes 3932168 | tf_op jit(solution)/shard_map/ppermute | solution.py:168
  431.7 79.0 %collective-permute-start.44 = (bf16[512,1280]{1,0:T(8,128)(2,1)S(1)}, bf16[512,1280]{1,0:T(8,128)(2,1)S(1)}, u32[]{:S(2)}, u32[]{:S(2)}) collective-permute-start(bf16[512,1280]{1,0:T(8,128)(2,1)S(1)} %maximum_maximum_fusion), channel_id=1, source_target_pairs={{0,8},{4,12},{8,0},{12,4},{16,24},{20,28},{24,16},{28,20},{1,9},{5... | collective-permute-start | bytes 3932168 | tf_op jit(solution)/shard_map/ppermute | solution.py:168
  455.8 56.9 %collective-permute-start.63 = (bf16[256,1280]{1,0:T(8,128)(2,1)S(1)}, bf16[256,1280]{1,0:T(8,128)(2,1)}, u32[]{:S(2)}, u32[]{:S(2)}) collective-permute-start(bf16[256,1280]{1,0:T(8,128)(2,1)S(1)} %pad_maximum_fusion.11), channel_id=1, source_target_pairs={{0,16},{4,20},{8,24},{12,28},{16,0},{20,4},{24,8},{28,12},{1,17},{... | collective-permute-start | bytes 1966088 | tf_op jit(solution)/shard_map/ppermute | solution.py:168
  510.7 32.5 %collective-permute-start.54 = (bf16[256,1280]{1,0:T(8,128)(2,1)}, bf16[256,1280]{1,0:T(8,128)(2,1)}, u32[]{:S(2)}, u32[]{:S(2)}) collective-permute-start(bf16[256,1280]{1,0:T(8,128)(2,1)} %pad_maximum_fusion.9), channel_id=1, source_target_pairs={{0,16},{4,20},{8,24},{12,28},{16,0},{20,4},{24,8},{28,12},{1,17},{... | collective-permute-start | bytes 1966088 | tf_op jit(solution)/shard_map/ppermute | solution.py:168
  512.7 71.2 %collective-permute-start.45 = (bf16[256,1280]{1,0:T(8,128)(2,1)}, bf16[256,1280]{1,0:T(8,128)(2,1)}, u32[]{:S(2)}, u32[]{:S(2)}) collective-permute-start(bf16[256,1280]{1,0:T(8,128)(2,1)} %pad_maximum_fusion.7), channel_id=1, source_target_pairs={{0,16},{4,20},{8,24},{12,28},{16,0},{20,4},{24,8},{28,12},{1,17},{... | collective-permute-start | bytes 1966088 | tf_op jit(solution)/shard_map/ppermute | solution.py:168
  513.8 43.0 %collective-permute-start.55 = (bf16[256,1280]{1,0:T(8,128)(2,1)}, bf16[256,1280]{1,0:T(8,128)(2,1)}, u32[]{:S(2)}, u32[]{:S(2)}) collective-permute-start(bf16[256,1280]{1,0:T(8,128)(2,1)} %slice.318), channel_id=1, source_target_pairs={{0,16},{4,20},{8,24},{12,28},{16,0},{20,4},{24,8},{28,12},{1,17},{... | collective-permute-start | bytes 1966088 | tf_op jit(solution)/shard_map/ppermute | solution.py:168
  528.5 55.3 %collective-permute-start.46 = (bf16[256,1280]{1,0:T(8,128)(2,1)}, bf16[256,1280]{1,0:T(8,128)(2,1)S(1)}, u32[]{:S(2)}, u32[]{:S(2)}) collective-permute-start(bf16[256,1280]{1,0:T(8,128)(2,1)} %slice.315), channel_id=1, source_target_pairs={{0,16},{4,20},{8,24},{12,28},{16,0},{20,4},{24,8},{28,12},{1,17},{... | collective-permute-start | bytes 1966088 | tf_op jit(solution)/shard_map/ppermute | solution.py:168
  (87 other events, 1837.6 us)

commit v2 on v1

--- a/solution.py
+++ b/solution.py
@@ -75,18 +75,18 @@
     return out.reshape(layers * strips * width, wide)
 
 
-def second_kernel(groups, layers, place, chips, *refs):
+def second_kernel(groups, parts, layers, place, chips, *refs):
     lhs = refs[:groups]
-    rhs = refs[groups : groups + layers]
-    gap_rows, gap_cols = refs[groups + layers], refs[groups + layers + 1]
+    rhs = refs[groups : groups + len(parts)]
+    gap_rows, gap_cols = refs[groups + len(parts)], refs[groups + len(parts) + 1]
     out_ref, left, right = refs[-3], refs[-2], refs[-1]
     dims = (((1,), (1,)), ((), ()))
     width = rhs[0].shape[0]
 
     @pl.when(pl.program_id(0) == 0)
     def _():
-        for n in range(layers):
-            right[pl.ds(pl.multiple_of(chips[n] * width, 32), width), :] = rhs[n][...]
+        for ref, (n, lo) in zip(rhs, parts):
+            right[pl.ds(pl.multiple_of(chips[n] * width + lo, 32), ref.shape[0]), :] = ref[...]
 
     start = 0
     for part in lhs:
@@ -104,13 +104,14 @@
         out_ref[:, n : n + pick] = (-total / (rows + gap_cols[:, n : n + pick])).astype(out_ref.dtype)
 
 
-def second_product(lhs, rhs, gap_rows, gap_cols, place, chips, strips, out, shape):
-    layers = len(rhs)
+def second_product(lhs, rhs, gap_rows, gap_cols, place, chips, strips, layers, out, shape):
+    parts = [(n, lo) for _, n, lo in rhs]
+    rhs = [x for x, _, _ in rhs]
     width, naux = rhs[0].shape
     tall = layers * width
     lhs = [x.reshape(layers, strips, width, x.shape[1]) for x in lhs]
     in_specs = [pl.BlockSpec((layers, 1, width, x.shape[3]), lambda i, a, b: (0, i, 0, 0)) for x in lhs]
-    in_specs += [pl.BlockSpec((width, naux), lambda i, a, b: (0, 0)) for x in rhs]
+    in_specs += [pl.BlockSpec((min(width, x.shape[0]), naux), lambda i, a, b: (0, 0)) for x in rhs]
     in_specs += [
         pl.BlockSpec((1, tall), lambda i, a, b: (0, a[0] * strips + i)),
         pl.BlockSpec((1, tall), lambda i, a, b: (0, a[1])),
@@ -129,7 +130,7 @@
         scratch_shapes=[pltpu.VMEM((tall, naux), BF), pltpu.VMEM((tall, naux), BF)],
     )
     return pl.pallas_call(
-        functools.partial(second_kernel, len(lhs), layers),
+        functools.partial(second_kernel, len(lhs), parts, layers),
         out_shape=jax.ShapeDtypeStruct(shape, BF),
         grid_spec=grid_spec,
         input_output_aliases=aliases,
@@ -140,6 +141,65 @@
         ),
         name="second",
     )(place, chips, *operands)
+
+
+def choose_kernel(count, start, owners, *refs):
+    early, late = refs[:count], refs[count : 2 * count]
+    first, second, own, sems = refs[2 * count :]
+    width, wide = own.shape[0], early[0].shape[1]
+    cut = width // 2
+    plan = [
+        (0, 0, width, own, 0),
+        (1, 0, width, first, 0),
+        (2, 0, width, second, 0),
+        (3, 0, cut, first, width),
+        (3, cut, cut, second, width),
+    ]
+
+    def copies(n, i):
+        _, lo, tall, out, at = plan[n]
+        rest = late[i].shape[1]
+        return (
+            pltpu.make_async_copy(
+                early[i].at[pl.ds(start + lo, tall), :],
+                out.at[pl.ds(at, tall), pl.ds(0, wide)],
+                sems.at[2 * n],
+            ),
+            pltpu.make_async_copy(
+                late[i].at[pl.ds(lo, tall), :],
+                out.at[pl.ds(at, tall), pl.ds(wide, rest)],
+                sems.at[2 * n + 1],
+            ),
+        )
+
+    for n in range(len(plan)):
+        for i in range(count):
+
+            @pl.when(owners[plan[n][0]] == i)
+            def _(n=n, i=i):
+                for copy in copies(n, i):
+                    copy.start()
+
+    for n in range(len(plan)):
+        for copy in copies(n, 0):
+            copy.wait()
+
+
+def choose(owners, early, late, start):
+    width = late[0].shape[0]
+    naux = early[0].shape[1] + late[0].shape[1]
+    both = width + width // 2
+    any_spec = pl.BlockSpec(memory_space=pl.ANY)
+    vmem_spec = pl.BlockSpec(memory_space=pltpu.VMEM)
+    return pl.pallas_call(
+        functools.partial(choose_kernel, len(early), start),
+        out_shape=[jax.ShapeDtypeStruct((rows, naux), BF) for rows in (both, both, width)],
+        in_specs=[pl.BlockSpec(memory_space=pltpu.SMEM)] + [any_spec] * (2 * len(early)),
+        out_specs=[vmem_spec] * 3,
+        scratch_shapes=[pltpu.SemaphoreType.DMA((10,))],
+        cost_estimate=pl.CostEstimate(flops=0, bytes_accessed=16 * width * naux, transcendentals=0),
+        name="choose",
+    )(owners, *early, *late)
 
 
 def body(layers, amplitudes, cholesky, occ_map, vir_map):
@@ -235,25 +295,22 @@
     for s in range(strips):
         at = slice(s * width, (s + 1) * width)
         late = line(shares[-1][at])
-        ahead, late = lax.optimization_barrier((early, late))
-        rows = [[x[at] for x in group] for group in ahead] + [late]
-
-        def block(d, rows=rows):
-            owner = jnp.bitwise_xor(k, d) - c + layers - 1
-            return jnp.concatenate([lax.select_n(owner, *group) for group in rows], axis=1)
-
-        blocks = [block(d) for d in range(layers)]
-        pair = jnp.concatenate([blocks[1], blocks[-1]])
-        if layers == 4:
-            one = across(pair, 1)
-            two = across(blocks[2], 2)
-            rest = one[width:]
-            rhs = [blocks[0], one, two, across(rest, 2)]
+        owners = (chips - c + layers - 1).astype(jnp.int32)
+        if layers == 4 and len(early) == 1:
+            one, two, own = choose(owners, early[0], late, s * width)
+            one, two = across(one, 1), across(two, 2)
+            rest, more = one[width:], two[width:]
+            rest, more = across(rest, 2), across(more, 1)
+            rhs = [(own, 0, 0), (one, 1, 0), (two, 2, 0), (rest, 3, 0), (more, 3, width // 2)]
         else:
-            rhs = [blocks[0]] + [across(blocks[d], d) for d in range(1, layers)]
+            rows = [[x[at] for x in group] for group in early] + [late]
+            blocks = [
+                jnp.concatenate([lax.select_n(owners[d], *group) for group in rows], axis=1) for d in range(layers)
+            ]
+            rhs = [(blocks[0], 0, 0)] + [(across(blocks[d], d), d, 0) for d in range(1, layers)]
         shape = (tile_rows, tile_cols)
-        out = second_product(near, rhs, gap_rows, gap_cols, near_at(s), sides, strips, out, shape)
-        out = second_product(far, rhs, gap_rows, gap_cols, far_at(s), sides, strips, out, shape)
+        out = second_product(near, rhs, gap_rows, gap_cols, near_at(s), sides, strips, layers, out, shape)
+        out = second_product(far, rhs, gap_rows, gap_cols, far_at(s), sides, strips, layers, out, shape)
     return out
 
 

time: 614 us -> 604 us (0.984)
  other arithmetic: 43.1 us -> 26.4 us
  Pallas kernels: 165 us -> 177 us
    ppermute x18, waiting for transfers between devices: 99.9 us -> 135 us  [line(): downs.append(lax.ppermute(downs[-1], 'col', down))]
    ppermute x25 -> x28, waiting for transfers between devices: 152 us -> 131 us  [across(): return lax.ppermute(x, 'row', [(n, n ^ 2 * d) for n in range(2 * layers)])]
    ppermute x18, waiting for transfers between devices: 46 us -> 26.2 us  [line(): ups.append(lax.ppermute(ups[-1], 'col', up))]
    pallas_call x6 -> x9, Pallas kernels: 81.7 us -> 93.3 us  [the longest x6 81.5 us: second_product(): pl.pallas_call(functools.partial(second_kernel, len(lhs), parts, layers),...]
    select_n x18 -> x0, other arithmetic: 9.63 us -> none  [block(): lax.select_n(owner, *group)]
    slice x3 -> x6, local copies, waits for them, and re-layouts: 1.89 us -> 8.84 us  [body(): rest, more = (one[width:], two[width:])]
    ppermute x25 -> x28, starting transfers between devices: 28 us -> 28.8 us  [across(): return lax.ppermute(x, 'row', [(n, n ^ 2 * d) for n in range(2 * layers)])]
  transfers between devices with their start and end apart: 65 -> 68, of which waited for: 30 -> 32; matrix products, arithmetic and copies ran while one was open for 8% -> 6% of each run, Pallas kernels for 23% -> 25%
where the time goes in v2:
time: 604 us; the launch traced here: 601 us
  waiting for transfers between devices  292 us (48%)
  Pallas kernels  177 us (29%)
  starting transfers between devices  86.7 us (14%)
  other arithmetic  26.4 us (4%)
  local copies, waits for them, and re-layouts  18.3 us (3%)
    ppermute x18, waiting for transfers between devices, line(): downs.append(lax.ppermute(downs[-1], 'col', down))  135 us
    ppermute x28, waiting for transfers between devices, across(): return lax.ppermute(x, 'row', [(n, n ^ 2 * d) for n in range(2 * layers)])  131 us
    pallas_call x4, Pallas kernels, first_product(): pl.pallas_call(functools.partial(first_kernel, keep), out_shape=jax.Shape...  83.6 us
    pallas_call x6, Pallas kernels, second_product(): pl.pallas_call(functools.partial(second_kernel, len(lhs), parts, layers),...  81.5 us
    ppermute x18, starting transfers between devices, line(): ups.append(lax.ppermute(ups[-1], 'col', up))  34.6 us
    ppermute x28, starting transfers between devices, across(): return lax.ppermute(x, 'row', [(n, n ^ 2 * d) for n in range(2 * layers)])  28.8 us
    ppermute x18, waiting for transfers between devices, line(): ups.append(lax.ppermute(ups[-1], 'col', up))  26.2 us
    ppermute x18, starting transfers between devices, line(): downs.append(lax.ppermute(downs[-1], 'col', down))  23.3 us
  transfers between devices with their start and end apart: 68, of which 32 were waited for; matrix products, arithmetic and copies ran while one was open for 6% of the time, Pallas kernels for 25%

profile of v2, /device:TPU:0, one launch (start us, length us, event | category | flops | bytes accessed | tf_op | source)
XLA Modules:
  0.0 601.4 jit_solution(4436135430419776225)
XLA Ops:
  7.7 23.8 %collective-permute-done.16.refs_2_ = bf16[768,768]{1,0:T(8,128)(2,1)S(1)} collective-permute-done((bf16[768,768]{1,0:T(8,128)(2,1)S(1)}, bf16[768,768]{1,0:T(8,128)(2,1)S(1)}, u32[]{:S(2)}, u32[]{:S(2)}) %collective-permute-start.16) | collective-permute-done | bytes 1179680 | tf_op jit(solution)/shard_map/ppermute | solution.py:223
  38.7 26.6 %collective-permute-done.20.refs_5_ = bf16[768,768]{1,0:T(8,128)(2,1)} collective-permute-done((bf16[768,768]{1,0:T(8,128)(2,1)S(1)}, bf16[768,768]{1,0:T(8,128)(2,1)}, u32[]{:S(2)}, u32[]{:S(2)}) %collective-permute-start.20) | collective-permute-done | bytes 1179680 | tf_op jit(solution)/shard_map/ppermute | solution.py:224
  76.9 19.5 %collective-permute-done.21.refs_6_ = bf16[768,768]{1,0:T(8,128)(2,1)} collective-permute-done((bf16[768,768]{1,0:T(8,128)(2,1)}, bf16[768,768]{1,0:T(8,128)(2,1)}, u32[]{:S(2)}, u32[]{:S(2)}) %collective-permute-start.21) | collective-permute-done | bytes 1179680 | tf_op jit(solution)/shard_map/ppermute | solution.py:224
  96.4 23.5 %first.7 = f32[4,3,256,768]{3,2,1,0:T(8,128)} custom-call(s32[8]{0:T(128)} %pad_add_fusion.7.spots, s32[6]{0:T(128)} %pad_add_fusion.6.chips, bf16[6144,3072]{1,0:T(8,128)(2,1)} %t_ref.7, bf16[768,768]{1,0:T(8,128)(2,1)} %collective-permute-done.18.refs_0_, bf16[768,768]{1,0:T(8,128)(2,1)} %collective-permute-done.17.refs_1_, bf16[768,768]{1,0:T(8,128)(2,1)} %copy-done.11, ...), custom_call_target="tpu_custom_call" | custom-call | flops 14495514624 | bytes 28311552 | tf_op jit(solution)/shard_map/first/pallas_call | solution.py:64
  122.7 20.0 %collective-permute-done.4.refs_5_ = bf16[768,512]{1,0:T(8,128)(2,1)S(1)} collective-permute-done((bf16[768,512]{1,0:T(8,128)(2,1)}, bf16[768,512]{1,0:T(8,128)(2,1)S(1)}, u32[]{:S(2)}, u32[]{:S(2)}) %collective-permute-start.4) | collective-permute-done | bytes 786464 | tf_op jit(solution)/shard_map/ppermute | solution.py:224
  144.2 19.5 %collective-permute-done.5.refs_6_ = bf16[768,512]{1,0:T(8,128)(2,1)S(1)} collective-permute-done((bf16[768,512]{1,0:T(8,128)(2,1)S(1)}, bf16[768,512]{1,0:T(8,128)(2,1)S(1)}, u32[]{:S(2)}, u32[]{:S(2)}) %collective-permute-start.5) | collective-permute-done | bytes 786464 | tf_op jit(solution)/shard_map/ppermute | solution.py:224
  164.6 18.3 %first.5 = f32[4,3,256,512]{3,2,1,0:T(8,128)} custom-call(s32[8]{0:T(128)} %pad_add_fusion.7.spots, s32[6]{0:T(128)} %pad_add_fusion.6.chips, bf16[6144,3072]{1,0:T(8,128)(2,1)} %t_ref.7, bf16[768,512]{1,0:T(8,128)(2,1)} %copy-done.15, bf16[768,512]{1,0:T(8,128)(2,1)} %copy-done.13, bf16[768,512]{1,0:T(8,128)(2,1)} %collective-permute-done.refs_2_, ...), custom_call_target="tpu_custom_call" | custom-call | flops 9663676416 | bytes 25165824 | tf_op jit(solution)/shard_map/first/pallas_call | solution.py:64
  182.8 18.3 %first.4 = f32[4,3,256,512]{3,2,1,0:T(8,128)} custom-call(s32[8]{0:T(128)} %pad_add_fusion.7.spots, s32[6]{0:T(128)} %pad_add_fusion.6.chips, bf16[6144,3072]{1,0:T(8,128)(2,1)} %t_ref.7, bf16[768,512]{1,0:T(8,128)(2,1)} %copy-done.15, bf16[768,512]{1,0:T(8,128)(2,1)} %copy-done.13, bf16[768,512]{1,0:T(8,128)(2,1)} %collective-permute-done.refs_2_, ...), custom_call_target="tpu_custom_call" | custom-call | flops 9663676416 | bytes 25165824 | tf_op jit(solution)/shard_map/first/pallas_call | solution.py:64
  201.1 23.6 %first.6 = f32[4,3,256,768]{3,2,1,0:T(8,128)} custom-call(s32[8]{0:T(128)} %pad_add_fusion.7.spots, s32[6]{0:T(128)} %pad_add_fusion.6.chips, bf16[6144,3072]{1,0:T(8,128)(2,1)} %t_ref.7, bf16[768,768]{1,0:T(8,128)(2,1)} %collective-permute-done.18.refs_0_, bf16[768,768]{1,0:T(8,128)(2,1)} %collective-permute-done.17.refs_1_, bf16[768,768]{1,0:T(8,128)(2,1)} %copy-done.11, ...), custom_call_target="tpu_custom_call" | custom-call | flops 14495514624 | bytes 28311552 | tf_op jit(solution)/shard_map/first/pallas_call | solution.py:64
  236.9 11.8 %collective-permute-done.8 = bf16[768,512]{1,0:T(8,128)(2,1)S(1)} collective-permute-done((bf16[768,512]{1,0:T(8,128)(2,1)S(1)}, bf16[768,512]{1,0:T(8,128)(2,1)S(1)}, u32[]{:S(2)}, u32[]{:S(2)}) %collective-permute-start.8) | collective-permute-done | bytes 786464 | tf_op jit(solution)/shard_map/ppermute | solution.py:228
  254.3 29.1 %collective-permute-done.10 = bf16[384,512]{1,0:T(8,128)(2,1)S(1)} collective-permute-done((bf16[384,512]{1,0:T(8,128)(2,1)S(1)}, bf16[384,512]{1,0:T(8,128)(2,1)S(1)}, u32[]{:S(2)}, u32[]{:S(2)}) %collective-permute-start.10) | collective-permute-done | bytes 393248 | tf_op jit(solution)/shard_map/ppermute | solution.py:228
  321.3 9.8 %collective-permute-done.36.refs_5_ = bf16[768,512]{1,0:T(8,128)(2,1)S(1)} collective-permute-done((bf16[768,512]{1,0:T(8,128)(2,1)S(1)}, bf16[768,512]{1,0:T(8,128)(2,1)S(1)}, u32[]{:S(2)}, u32[]{:S(2)}) %collective-permute-start.36) | collective-permute-done | bytes 786464 | tf_op jit(solution)/shard_map/ppermute | solution.py:224
  331.8 10.8 %collective-permute-done.27 = bf16[768,768]{1,0:T(8,128)(2,1)S(1)} collective-permute-done((bf16[768,768]{1,0:T(8,128)(2,1)S(1)}, bf16[768,768]{1,0:T(8,128)(2,1)S(1)}, u32[]{:S(2)}, u32[]{:S(2)}) %collective-permute-start.27) | collective-permute-done | bytes 1179680 | tf_op jit(solution)/shard_map/ppermute | solution.py:228
  343.9 10.6 %collective-permute-done.12 = bf16[768,512]{1,0:T(8,128)(2,1)S(1)} collective-permute-done((bf16[768,512]{1,0:T(8,128)(2,1)S(1)}, bf16[768,512]{1,0:T(8,128)(2,1)S(1)}, u32[]{:S(2)}, u32[]{:S(2)}) %collective-permute-start.12) | collective-permute-done | bytes 786464 | tf_op jit(solution)/shard_map/ppermute | solution.py:228
  389.5 7.3 %collective-permute-done.41.refs_11_ = bf16[256,768]{1,0:T(8,128)(2,1)S(1)} collective-permute-done((bf16[256,768]{1,0:T(8,128)(2,1)S(1)}, bf16[256,768]{1,0:T(8,128)(2,1)S(1)}, u32[]{:S(2)}, u32[]{:S(2)}) %collective-permute-start.41) | collective-permute-done | bytes 393248 | tf_op jit(solution)/shard_map/ppermute | solution.py:224
  451.4 12.6 %collective-permute-done.64.refs_3_ = bf16[384,1280]{1,0:T(8,128)(2,1)} collective-permute-done((bf16[384,1280]{1,0:T(8,128)(2,1)}, bf16[384,1280]{1,0:T(8,128)(2,1)}, u32[]{:S(2)}, u32[]{:S(2)}) %collective-permute-start.64) | collective-permute-done | bytes 983072 | tf_op jit(solution)/shard_map/ppermute | solution.py:228
  465.9 19.1 %collective-permute-done.54.refs_3_ = bf16[384,1280]{1,0:T(8,128)(2,1)} collective-permute-done((bf16[384,1280]{1,0:T(8,128)(2,1)}, bf16[384,1280]{1,0:T(8,128)(2,1)}, u32[]{:S(2)}, u32[]{:S(2)}) %collective-permute-start.54) | collective-permute-done | bytes 983072 | tf_op jit(solution)/shard_map/ppermute | solution.py:228
  491.6 12.7 %collective-permute-done.44.refs_3_ = bf16[384,1280]{1,0:T(8,128)(2,1)} collective-permute-done((bf16[384,1280]{1,0:T(8,128)(2,1)}, bf16[384,1280]{1,0:T(8,128)(2,1)}, u32[]{:S(2)}, u32[]{:S(2)}) %collective-permute-start.44) | collective-permute-done | bytes 983072 | tf_op jit(solution)/shard_map/ppermute | solution.py:228
  518.5 13.6 %second.6.refs_9_ = bf16[6144,3072]{1,0:T(8,128)(2,1)} custom-call(s32[2]{0:T(128)} %pad_add_fusion.4.place, s32[6]{0:T(128)} %pad_add_fusion.6.chips, bf16[4,3,256,512]{3,2,1,0:T(8,128)(2,1)} %bitcast.17, bf16[4,3,256,768]{3,2,1,0:T(8,128)(2,1)} %bitcast.12.refs_1_, bf16[256,1280]{1,0:T(8,128)(2,1)} %get-tuple-element.60.refs_2_, ...), custom_call_target="tpu_custom_call" | custom-call | flops 8053063680 | bytes 14155776 | tf_op jit(solution)/shard_map/second/pallas_call | solution.py:132
  532.7 13.6 %second.7.refs_9_ = bf16[6144,3072]{1,0:T(8,128)(2,1)} custom-call(s32[2]{0:T(128)} %pad_add_fusion.5.place, s32[6]{0:T(128)} %pad_add_fusion.6.chips, bf16[4,3,256,512]{3,2,1,0:T(8,128)(2,1)} %bitcast.5.refs_0_, bf16[4,3,256,768]{3,2,1,0:T(8,128)(2,1)} %bitcast.8.refs_1_, ...), custom_call_target="tpu_custom_call", output_to_operand_aliasing={{}: (11, {})} | custom-call | flops 8053063680 | bytes 14155776 | tf_op jit(solution)/shard_map/second/pallas_call | solution.py:132
  546.3 13.6 %second.8.refs_9_ = bf16[6144,3072]{1,0:T(8,128)(2,1)} custom-call(s32[2]{0:T(128)} %pad_add_fusion.2.place, s32[6]{0:T(128)} %pad_add_fusion.6.chips, bf16[4,3,256,512]{3,2,1,0:T(8,128)(2,1)} %bitcast.18, bf16[4,3,256,768]{3,2,1,0:T(8,128)(2,1)} %bitcast.12.refs_1_, bf16[256,1280]{1,0:T(8,128)(2,1)} %get-tuple-element.57.refs_2_, ...), custom_call_target="tpu_custom_call", output_to_operand_aliasing={{}: (11, {})} | custom-call | flops 8053063680 | bytes 14155776 | tf_op jit(solution)/shard_map/second/pallas_call | solution.py:132
  559.9 13.6 %second.9.refs_9_ = bf16[6144,3072]{1,0:T(8,128)(2,1)} custom-call(s32[2]{0:T(128)} %pad_add_fusion.3.place, s32[6]{0:T(128)} %pad_add_fusion.6.chips, bf16[4,3,256,512]{3,2,1,0:T(8,128)(2,1)} %bitcast.5.refs_0_, bf16[4,3,256,768]{3,2,1,0:T(8,128)(2,1)} %bitcast.8.refs_1_, ...), custom_call_target="tpu_custom_call", output_to_operand_aliasing={{}: (11, {})} | custom-call | flops 8053063680 | bytes 14155776 | tf_op jit(solution)/shard_map/second/pallas_call | solution.py:132
  574.2 13.6 %second.10.refs_9_ = bf16[6144,3072]{1,0:T(8,128)(2,1)} custom-call(s32[2]{0:T(128)} %get-tuple-element.86.place, s32[6]{0:T(128)} %pad_add_fusion.6.chips, bf16[4,3,256,512]{3,2,1,0:T(8,128)(2,1)} %bitcast.19, bf16[4,3,256,768]{3,2,1,0:T(8,128)(2,1)} %bitcast.12.refs_1_, ...), custom_call_target="tpu_custom_call", output_to_operand_aliasing={{}: (11, {})} | custom-call | flops 8053063680 | bytes 14155776 | tf_op jit(solution)/shard_map/second/pallas_call | solution.py:132
  587.8 13.6 %second.11 = bf16[6144,3072]{1,0:T(8,128)(2,1)} custom-call(s32[2]{0:T(128)} %get-tuple-element.87.place, s32[6]{0:T(128)} %pad_add_fusion.6.chips, bf16[4,3,256,512]{3,2,1,0:T(8,128)(2,1)} %bitcast.5.refs_0_, bf16[4,3,256,768]{3,2,1,0:T(8,128)(2,1)} %bitcast.8.refs_1_, ...), custom_call_target="tpu_custom_call", output_to_operand_aliasing={{}: (11, {})} | custom-call | flops 8053063680 | bytes 14155776 | tf_op jit(solution)/shard_map/second/pallas_call | solution.py:132
  (247 shorter events, 202.1 us)
Async XLA Ops:
  1.4 30.2 %collective-permute-start.16 = (bf16[768,768]{1,0:T(8,128)(2,1)S(1)}, bf16[768,768]{1,0:T(8,128)(2,1)S(1)}, u32[]{:S(2)}, u32[]{:S(2)}) collective-permute-start(bf16[768,768]{1,0:T(8,128)(2,1)S(1)} %slice.190.refs_3_), channel_id=1, source_target_pairs={{0,1},{1,2},{2,3},{4,5},{5,6},{6,7},{8,9},{9,10},{10,11},{12,13},{... | collective-permute-start | bytes 3538952 | tf_op jit(solution)/shard_map/ppermute | solution.py:223
  37.0 39.9 %collective-permute-start.18 = (bf16[768,768]{1,0:T(8,128)(2,1)}, bf16[768,768]{1,0:T(8,128)(2,1)}, u32[]{:S(2)}, u32[]{:S(2)}) collective-permute-start(bf16[768,768]{1,0:T(8,128)(2,1)} %collective-permute-done.17.refs_1_), channel_id=1, source_target_pairs={{2,3},{6,7},{10,11},{14,15},{18,19},{22,23},{26,27},{30,31}} | collective-permute-start | bytes 3538952 | tf_op jit(solution)/shard_map/ppermute | solution.py:223
  65.4 31.0 %collective-permute-start.21 = (bf16[768,768]{1,0:T(8,128)(2,1)}, bf16[768,768]{1,0:T(8,128)(2,1)}, u32[]{:S(2)}, u32[]{:S(2)}) collective-permute-start(bf16[768,768]{1,0:T(8,128)(2,1)} %collective-permute-done.20.refs_5_), channel_id=1, source_target_pairs={{1,0},{5,4},{9,8},{13,12},{17,16},{21,20},{25,24},{29,28}} | collective-permute-start | bytes 3538952 | tf_op jit(solution)/shard_map/ppermute | solution.py:224
  67.9 52.1 %collective-permute-start = (bf16[768,512]{1,0:T(8,128)(2,1)S(1)}, bf16[768,512]{1,0:T(8,128)(2,1)}, u32[]{:S(2)}, u32[]{:S(2)}) collective-permute-start(bf16[768,512]{1,0:T(8,128)(2,1)S(1)} %slice.167.refs_3_), channel_id=1, source_target_pairs={{0,1},{1,2},{2,3},{4,5},{5,6},{6,7},{8,9},{9,10},{10,11},{12,13},{... | collective-permute-start | bytes 2359304 | tf_op jit(solution)/shard_map/ppermute | solution.py:223
  74.3 46.4 %collective-permute-start.3 = (bf16[768,512]{1,0:T(8,128)(2,1)S(1)}, bf16[768,512]{1,0:T(8,128)(2,1)}, u32[]{:S(2)}, u32[]{:S(2)}) collective-permute-start(bf16[768,512]{1,0:T(8,128)(2,1)S(1)} %slice.167.refs_3_), channel_id=1, source_target_pairs={{3,2},{2,1},{1,0},{7,6},{6,5},{5,4},{11,10},{10,9},{9,8},{15,14},{... | collective-permute-start | bytes 2359304 | tf_op jit(solution)/shard_map/ppermute | solution.py:224
  119.9 111.5 %collective-permute-start.22 = (f32[3072,768]{1,0:T(8,128)}, f32[3072,768]{1,0:T(8,128)}, u32[]{:S(2)}, u32[]{:S(2)}) collective-permute-start(f32[3072,768]{1,0:T(8,128)} %bitcast.26), channel_id=1, source_target_pairs={{0,4},{4,0},{8,12},{12,8},{16,20},{20,16},{24,28},{28,24},{1,5},{5... | collective-permute-start | bytes 28311560 | tf_op jit(solution)/shard_map/ppermute | solution.py:231
  182.8 41.9 %collective-permute-start.6 = (f32[3072,512]{1,0:T(8,128)}, f32[3072,512]{1,0:T(8,128)}, u32[]{:S(2)}, u32[]{:S(2)}) collective-permute-start(f32[3072,512]{1,0:T(8,128)} %bitcast.27), channel_id=1, source_target_pairs={{0,4},{4,0},{8,12},{12,8},{16,20},{20,16},{24,28},{28,24},{1,5},{5... | collective-permute-start | bytes 18874376 | tf_op jit(solution)/shard_map/ppermute | solution.py:231
  234.8 48.6 %collective-permute-start.24 = (bf16[768,768]{1,0:T(8,128)(2,1)S(1)}, bf16[768,768]{1,0:T(8,128)(2,1)S(1)}, u32[]{:S(2)}, u32[]{:S(2)}) collective-permute-start(bf16[768,768]{1,0:T(8,128)(2,1)S(1)} %pad_maximum_fusion.2), channel_id=1, source_target_pairs={{0,16},{4,20},{8,24},{12,28},{16,0},{20,4},{24,8},{28,12},{1,17},{... | collective-permute-start | bytes 3538952 | tf_op jit(solution)/shard_map/ppermute | solution.py:228
  235.4 47.9 %collective-permute-start.23 = (bf16[768,768]{1,0:T(8,128)(2,1)S(1)}, bf16[768,768]{1,0:T(8,128)(2,1)S(1)}, u32[]{:S(2)}, u32[]{:S(2)}) collective-permute-start(bf16[768,768]{1,0:T(8,128)(2,1)S(1)} %pad_maximum_fusion.1), channel_id=1, source_target_pairs={{0,8},{4,12},{8,0},{12,4},{16,24},{20,28},{24,16},{28,20},{1,9},{5... | collective-permute-start | bytes 3538952 | tf_op jit(solution)/shard_map/ppermute | solution.py:228
  252.2 31.1 %collective-permute-start.10 = (bf16[384,512]{1,0:T(8,128)(2,1)S(1)}, bf16[384,512]{1,0:T(8,128)(2,1)S(1)}, u32[]{:S(2)}, u32[]{:S(2)}) collective-permute-start(bf16[384,512]{1,0:T(8,128)(2,1)S(1)} %get-tuple-element.77), channel_id=1, source_target_pairs={{0,8},{4,12},{8,0},{12,4},{16,24},{20,28},{24,16},{28,20},{1,9},{5... | collective-permute-start | bytes 1179656 | tf_op jit(solution)/shard_map/ppermute | solution.py:228
  307.3 35.3 %collective-permute-start.27 = (bf16[768,768]{1,0:T(8,128)(2,1)S(1)}, bf16[768,768]{1,0:T(8,128)(2,1)S(1)}, u32[]{:S(2)}, u32[]{:S(2)}) collective-permute-start(bf16[768,768]{1,0:T(8,128)(2,1)S(1)} %pad_maximum_fusion), channel_id=1, source_target_pairs={{0,8},{4,12},{8,0},{12,4},{16,24},{20,28},{24,16},{28,20},{1,9},{5... | collective-permute-start | bytes 3538952 | tf_op jit(solution)/shard_map/ppermute | solution.py:228
  308.8 47.2 %collective-permute-start.28 = (bf16[768,768]{1,0:T(8,128)(2,1)S(1)}, bf16[768,768]{1,0:T(8,128)(2,1)S(1)}, u32[]{:S(2)}, u32[]{:S(2)}) collective-permute-start(bf16[768,768]{1,0:T(8,128)(2,1)S(1)} %pad_maximum_fusion), channel_id=1, source_target_pairs={{0,16},{4,20},{8,24},{12,28},{16,0},{20,4},{24,8},{28,12},{1,17},{... | collective-permute-start | bytes 3538952 | tf_op jit(solution)/shard_map/ppermute | solution.py:228
  319.2 35.4 %collective-permute-start.12 = (bf16[768,512]{1,0:T(8,128)(2,1)S(1)}, bf16[768,512]{1,0:T(8,128)(2,1)S(1)}, u32[]{:S(2)}, u32[]{:S(2)}) collective-permute-start(bf16[768,512]{1,0:T(8,128)(2,1)S(1)} %pad_maximum_fusion.5.refs_3_), channel_id=1, source_target_pairs={{0,16},{4,20},{8,24},{12,28},{16,0},{20,4},{24,8},{28,12},{1,17},{... | collective-permute-start | bytes 2359304 | tf_op jit(solution)/shard_map/ppermute | solution.py:228
  320.7 42.2 %collective-permute-start.13 = (bf16[384,512]{1,0:T(8,128)(2,1)S(1)}, bf16[384,512]{1,0:T(8,128)(2,1)S(1)}, u32[]{:S(2)}, u32[]{:S(2)}) collective-permute-start(bf16[384,512]{1,0:T(8,128)(2,1)S(1)} %slice.230), channel_id=1, source_target_pairs={{0,16},{4,20},{8,24},{12,28},{16,0},{20,4},{24,8},{28,12},{1,17},{... | collective-permute-start | bytes 1179656 | tf_op jit(solution)/shard_map/ppermute | solution.py:228
  331.1 38.0 %collective-permute-start.34 = (bf16[768,512]{1,0:T(8,128)(2,1)S(1)}, bf16[768,512]{1,0:T(8,128)(2,1)S(1)}, u32[]{:S(2)}, u32[]{:S(2)}) collective-permute-start(bf16[768,512]{1,0:T(8,128)(2,1)S(1)} %collective-permute-done.33.refs_1_), channel_id=1, source_target_pairs={{2,3},{6,7},{10,11},{14,15},{18,19},{22,23},{26,27},{30,31}} | collective-permute-start | bytes 2359304 | tf_op jit(solution)/shard_map/ppermute | solution.py:223
  342.6 33.3 %collective-permute-start.37 = (bf16[768,512]{1,0:T(8,128)(2,1)S(1)}, bf16[768,512]{1,0:T(8,128)(2,1)S(1)}, u32[]{:S(2)}, u32[]{:S(2)}) collective-permute-start(bf16[768,512]{1,0:T(8,128)(2,1)S(1)} %collective-permute-done.36.refs_5_), channel_id=1, source_target_pairs={{1,0},{5,4},{9,8},{13,12},{17,16},{21,20},{25,24},{29,28}} | collective-permute-start | bytes 2359304 | tf_op jit(solution)/shard_map/ppermute | solution.py:224
  382.9 149.8 %collective-permute-start.31 = (bf16[3072,768]{1,0:T(8,128)(2,1)}, bf16[3072,768]{1,0:T(8,128)(2,1)}, u32[]{:S(2)}, u32[]{:S(2)}) collective-permute-start(bf16[3072,768]{1,0:T(8,128)(2,1)} %constant_dynamic-update-slice_fusion.6), channel_id=1, source_target_pairs={{0,4},{4,0},{8,12},{12,8},{16,20},{20,16},{24,28},{28,24},{1,5},{5... | collective-permute-start | bytes 14155784 | tf_op jit(solution)/shard_map/ppermute | solution.py:231
  430.5 101.6 %collective-permute-start.15 = (bf16[3072,512]{1,0:T(8,128)(2,1)S(1)}, bf16[3072,512]{1,0:T(8,128)(2,1)}, u32[]{:S(2)}, u32[]{:S(2)}) collective-permute-start(bf16[3072,512]{1,0:T(8,128)(2,1)S(1)} %constant_dynamic-update-slice_fusion), channel_id=1, source_target_pairs={{0,4},{4,0},{8,12},{12,8},{16,20},{20,16},{24,28},{28,24},{1,5},{5... | collective-permute-start | bytes 9437192 | tf_op jit(solution)/shard_map/ppermute | solution.py:231
  447.0 38.1 %collective-permute-start.54 = (bf16[384,1280]{1,0:T(8,128)(2,1)}, bf16[384,1280]{1,0:T(8,128)(2,1)}, u32[]{:S(2)}, u32[]{:S(2)}) collective-permute-start(bf16[384,1280]{1,0:T(8,128)(2,1)} %get-tuple-element.58), channel_id=1, source_target_pairs={{0,8},{4,12},{8,0},{12,4},{16,24},{20,28},{24,16},{28,20},{1,9},{5... | collective-permute-start | bytes 2949128 | tf_op jit(solution)/shard_map/ppermute | solution.py:228
  465.4 38.9 %collective-permute-start.44 = (bf16[384,1280]{1,0:T(8,128)(2,1)}, bf16[384,1280]{1,0:T(8,128)(2,1)}, u32[]{:S(2)}, u32[]{:S(2)}) collective-permute-start(bf16[384,1280]{1,0:T(8,128)(2,1)} %get-tuple-element.55), channel_id=1, source_target_pairs={{0,8},{4,12},{8,0},{12,4},{16,24},{20,28},{24,16},{28,20},{1,9},{5... | collective-permute-start | bytes 2949128 | tf_op jit(solution)/shard_map/ppermute | solution.py:228
  513.2 33.0 %collective-permute-start.56 = (bf16[128,1280]{1,0:T(8,128)(2,1)}, bf16[128,1280]{1,0:T(8,128)(2,1)}, u32[]{:S(2)}, u32[]{:S(2)}) collective-permute-start(bf16[128,1280]{1,0:T(8,128)(2,1)} %slice.247), channel_id=1, source_target_pairs={{0,16},{4,20},{8,24},{12,28},{16,0},{20,4},{24,8},{28,12},{1,17},{... | collective-permute-start | bytes 983048 | tf_op jit(solution)/shard_map/ppermute | solution.py:228
  516.4 29.9 %collective-permute-start.57 = (bf16[128,1280]{1,0:T(8,128)(2,1)}, bf16[128,1280]{1,0:T(8,128)(2,1)}, u32[]{:S(2)}, u32[]{:S(2)}) collective-permute-start(bf16[128,1280]{1,0:T(8,128)(2,1)} %slice.248), channel_id=1, source_target_pairs={{0,8},{4,12},{8,0},{12,4},{16,24},{20,28},{24,16},{28,20},{1,9},{5... | collective-permute-start | bytes 983048 | tf_op jit(solution)/shard_map/ppermute | solution.py:228
  517.9 55.6 %collective-permute-start.46 = (bf16[128,1280]{1,0:T(8,128)(2,1)}, bf16[128,1280]{1,0:T(8,128)(2,1)}, u32[]{:S(2)}, u32[]{:S(2)}) collective-permute-start(bf16[128,1280]{1,0:T(8,128)(2,1)} %slice.243), channel_id=1, source_target_pairs={{0,16},{4,20},{8,24},{12,28},{16,0},{20,4},{24,8},{28,12},{1,17},{... | collective-permute-start | bytes 983048 | tf_op jit(solution)/shard_map/ppermute | solution.py:228
  532.1 41.4 %collective-permute-start.47 = (bf16[128,1280]{1,0:T(8,128)(2,1)}, bf16[128,1280]{1,0:T(8,128)(2,1)S(1)}, u32[]{:S(2)}, u32[]{:S(2)}) collective-permute-start(bf16[128,1280]{1,0:T(8,128)(2,1)} %slice.244), channel_id=1, source_target_pairs={{0,8},{4,12},{8,0},{12,4},{16,24},{20,28},{24,16},{28,20},{1,9},{5... | collective-permute-start | bytes 983048 | tf_op jit(solution)/shard_map/ppermute | solution.py:228
  (81 other events, 1834.3 us)

commit v3 on v2

--- a/solution.py
+++ b/solution.py
@@ -95,13 +95,13 @@
             left[n * width : (n + 1) * width, start : start + wide] = part[chips[n], 0]
         start += wide
     broad = out_ref.shape[1]
-    pick = 512 if broad % 512 == 0 else broad
+    pick = 256 if broad % 256 == 0 else broad
     rows = jnp.transpose(jnp.broadcast_to(gap_rows[...], (LANES, gap_rows.shape[1])))[:, :1]
     for n in range(0, broad, pick):
         total = lax.dot_general(
             left[...], right[n : n + pick, :], dims, preferred_element_type=jnp.float32
         )
-        out_ref[:, n : n + pick] = (-total / (rows + gap_cols[:, n : n + pick])).astype(out_ref.dtype)
+        out_ref[:, n : n + pick] = (-total * (1.0 / (rows + gap_cols[:, n : n + pick]))).astype(out_ref.dtype)
 
 
 def second_product(lhs, rhs, gap_rows, gap_cols, place, chips, strips, layers, out, shape):
@@ -246,35 +246,40 @@
     )[None, :]
 
     shares = []
-    for lo, hi in spans:
+    for n, (lo, hi) in enumerate(spans):
         pieces = line(cholesky[:, lo:hi])
         sent = first_product(amplitudes, pieces, spots, sides, layers, strips, False)
         kept = first_product(amplitudes, pieces, spots, sides, layers, strips, True)
         came = swap(sent)
 
-        def both(d, part=None, kept=kept, came=came):
-            at = slice(d * piece, (d + 1) * piece)
-            if part is not None:
-                at = slice(d * piece + part * mid, d * piece + (part + 1) * mid)
+        def rows(d, lo, hi, kept=kept, came=came):
+            at = slice(d * piece + lo, d * piece + hi)
             return kept[at] + came[at]
 
         if layers == 4:
-            a0 = jnp.concatenate([both(1, 0), both(3, 0)]).astype(BF)
-            b0 = jnp.concatenate([both(2, 1), both(3, 1)]).astype(BF)
-            a1, b1 = across(a0, 1), across(b0, 2)
-            kept, came, a1, b1 = lax.optimization_barrier((kept, came, a1, b1))
-            a2 = (both(2, 0, kept, came) + a1[mid:].astype(F32)).astype(BF)
-            b2 = (both(1, 1, kept, came) + b1[mid:].astype(F32)).astype(BF)
-            a2, b2 = across(a2, 2), across(b2, 1)
-            kept, came, a1, b1, a2, b2 = lax.optimization_barrier((kept, came, a1, b1, a2, b2))
-            top = both(0, 0, kept, came) + a1[:mid].astype(F32) + a2.astype(F32)
-            low = both(0, 1, kept, came) + b1[:mid].astype(F32) + b2.astype(F32)
-            total = jnp.concatenate([top, low])
+            ends = [0, width, piece] if n == chunks - 1 and strips > 1 else [0, piece]
+            done = []
+            for lo, hi in zip(ends[:-1], ends[1:]):
+                cut = (lo + hi) // 2
+                tall = cut - lo
+                a0 = jnp.concatenate([rows(1, lo, cut, kept, came), rows(3, lo, cut, kept, came)]).astype(BF)
+                b0 = jnp.concatenate([rows(2, cut, hi, kept, came), rows(3, cut, hi, kept, came)]).astype(BF)
+                a1, b1 = across(a0, 1), across(b0, 2)
+                keep2, came2, a1, b1 = lax.optimization_barrier((kept, came, a1, b1))
+                a2 = (rows(2, lo, cut, keep2, came2) + a1[tall:].astype(F32)).astype(BF)
+                b2 = (rows(1, cut, hi, keep2, came2) + b1[tall:].astype(F32)).astype(BF)
+                a2, b2 = across(a2, 2), across(b2, 1)
+                keep2, came2, a1, b1, a2, b2 = lax.optimization_barrier((keep2, came2, a1, b1, a2, b2))
+                top = rows(0, lo, cut, keep2, came2) + a1[:tall].astype(F32) + a2.astype(F32)
+                low = rows(0, cut, hi, keep2, came2) + b1[:tall].astype(F32) + b2.astype(F32)
+                done.append(jnp.concatenate([top, low]).astype(BF))
+                kept, came, _, _ = lax.optimization_barrier((kept, came, a0, b0))
         else:
-            total = both(0)
+            total = rows(0, 0, piece)
             for d in range(1, layers):
-                total = total + across(both(d).astype(BF), d).astype(F32)
-        shares.append(total.astype(BF))
+                total = total + across(rows(d, 0, piece).astype(BF), d).astype(F32)
+            done = [total.astype(BF)]
+        shares.append(jnp.concatenate(done) if len(done) > 1 else done[0])
 
     splits = [(0, chunks - 1), (chunks - 1, chunks)] if chunks > 1 else [(0, 1)]
     near, far = [], []
@@ -291,10 +296,16 @@
     early = [line(x) for x in shares[:-1]]
     near_at = lambda s: jnp.stack([j, jnp.full_like(j, s)]).astype(jnp.int32)
     far_at = lambda s: jnp.stack([1 - j, jnp.full_like(j, s)]).astype(jnp.int32)
+
+    def strip_of(s):
+        if len(done) == 1:
+            return done[0][s * width : (s + 1) * width]
+        return done[0] if s == 0 else done[1][(s - 1) * width : s * width]
+
     out = None
     for s in range(strips):
         at = slice(s * width, (s + 1) * width)
-        late = line(shares[-1][at])
+        late = line(strip_of(s))
         owners = (chips - c + layers - 1).astype(jnp.int32)
         if layers == 4 and len(early) == 1:
             one, two, own = choose(owners, early[0], late, s * width)

time: 604 us -> 586 us (0.970)
  waiting for transfers between devices: 292 us -> 250 us
  starting transfers between devices: 86.7 us -> 104 us
  other arithmetic: 26.4 us -> 33.4 us
    ppermute x28 -> x32, waiting for transfers between devices: 131 us -> 89.3 us  [across(): return lax.ppermute(x, 'row', [(n, n ^ 2 * d) for n in range(2 * layers)])]
    ppermute x18, starting transfers between devices: 34.6 us -> 47.4 us  [line(): ups.append(lax.ppermute(ups[-1], 'col', up))]
    ppermute x28 -> x32, starting transfers between devices: 28.8 us -> 32.7 us  [across(): return lax.ppermute(x, 'row', [(n, n ^ 2 * d) for n in range(2 * layers)])]
  transfers between devices with their start and end apart: 68 -> 72, of which waited for: 32 -> 32; matrix products, arithmetic and copies ran while one was open for 6% -> 8% of each run, Pallas kernels for 25% -> 26%
where the time goes in v3:
time: 586 us; the launch traced here: 583 us
  waiting for transfers between devices  250 us (43%)
  Pallas kernels  177 us (30%)
  starting transfers between devices  104 us (18%)
  other arithmetic  33.4 us (6%)
  local copies, waits for them, and re-layouts  18.1 us (3%)
    ppermute x18, waiting for transfers between devices, line(): downs.append(lax.ppermute(downs[-1], 'col', down))  133 us
    ppermute x32, waiting for transfers between devices, across(): return lax.ppermute(x, 'row', [(n, n ^ 2 * d) for n in range(2 * layers)])  89.3 us
    pallas_call x4, Pallas kernels, first_product(): pl.pallas_call(functools.partial(first_kernel, keep), out_shape=jax.Shape...  83.6 us
    pallas_call x6, Pallas kernels, second_product(): pl.pallas_call(functools.partial(second_kernel, len(lhs), parts, layers),...  81.5 us
    ppermute x18, starting transfers between devices, line(): ups.append(lax.ppermute(ups[-1], 'col', up))  47.4 us
    ppermute x32, starting transfers between devices, across(): return lax.ppermute(x, 'row', [(n, n ^ 2 * d) for n in range(2 * layers)])  32.7 us
    ppermute x18, waiting for transfers between devices, line(): ups.append(lax.ppermute(ups[-1], 'col', up))  27.1 us
    ppermute x18, starting transfers between devices, line(): downs.append(lax.ppermute(downs[-1], 'col', down))  23.1 us
  transfers between devices with their start and end apart: 72, of which 32 were waited for; matrix products, arithmetic and copies ran while one was open for 8% of the time, Pallas kernels for 26%

profile of v3, /device:TPU:0, one launch (start us, length us, event | category | flops | bytes accessed | tf_op | source)
XLA Modules:
  0.0 582.9 jit_solution(7803263249151546498)
XLA Ops:
  7.7 23.8 %collective-permute-done.16.refs_2_ = bf16[768,768]{1,0:T(8,128)(2,1)S(1)} collective-permute-done((bf16[768,768]{1,0:T(8,128)(2,1)S(1)}, bf16[768,768]{1,0:T(8,128)(2,1)S(1)}, u32[]{:S(2)}, u32[]{:S(2)}) %collective-permute-start.16) | collective-permute-done | bytes 1179680 | tf_op jit(solution)/shard_map/ppermute | solution.py:223
  47.5 19.9 %collective-permute-done.20.refs_5_ = bf16[768,768]{1,0:T(8,128)(2,1)} collective-permute-done((bf16[768,768]{1,0:T(8,128)(2,1)S(1)}, bf16[768,768]{1,0:T(8,128)(2,1)}, u32[]{:S(2)}, u32[]{:S(2)}) %collective-permute-start.20) | collective-permute-done | bytes 1179680 | tf_op jit(solution)/shard_map/ppermute | solution.py:224
  70.2 14.0 %collective-permute-done.3.refs_4_ = bf16[768,512]{1,0:T(8,128)(2,1)} collective-permute-done((bf16[768,512]{1,0:T(8,128)(2,1)S(1)}, bf16[768,512]{1,0:T(8,128)(2,1)}, u32[]{:S(2)}, u32[]{:S(2)}) %collective-permute-start.3) | collective-permute-done | bytes 786464 | tf_op jit(solution)/shard_map/ppermute | solution.py:224
  88.4 36.0 %collective-permute-done.4.refs_5_ = bf16[768,512]{1,0:T(8,128)(2,1)} collective-permute-done((bf16[768,512]{1,0:T(8,128)(2,1)}, bf16[768,512]{1,0:T(8,128)(2,1)}, u32[]{:S(2)}, u32[]{:S(2)}) %collective-permute-start.4) | collective-permute-done | bytes 786464 | tf_op jit(solution)/shard_map/ppermute | solution.py:224
  125.7 23.5 %first.7 = f32[4,3,256,768]{3,2,1,0:T(8,128)} custom-call(s32[8]{0:T(128)} %pad_add_fusion.7.spots, s32[6]{0:T(128)} %pad_add_fusion.6.chips, bf16[6144,3072]{1,0:T(8,128)(2,1)} %t_ref.7, bf16[768,768]{1,0:T(8,128)(2,1)} %collective-permute-done.18.refs_0_, bf16[768,768]{1,0:T(8,128)(2,1)} %collective-permute-done.17.refs_1_, bf16[768,768]{1,0:T(8,128)(2,1)} %copy-done.11, ...), custom_call_target="tpu_custom_call" | custom-call | flops 14495514624 | bytes 28311552 | tf_op jit(solution)/shard_map/first/pallas_call | solution.py:64
  149.2 18.3 %first.5 = f32[4,3,256,512]{3,2,1,0:T(8,128)} custom-call(s32[8]{0:T(128)} %pad_add_fusion.7.spots, s32[6]{0:T(128)} %pad_add_fusion.6.chips, bf16[6144,3072]{1,0:T(8,128)(2,1)} %t_ref.7, bf16[768,512]{1,0:T(8,128)(2,1)} %collective-permute-done.2.refs_0_, bf16[768,512]{1,0:T(8,128)(2,1)} %collective-permute-done.1.refs_1_, ...), custom_call_target="tpu_custom_call" | custom-call | flops 9663676416 | bytes 25165824 | tf_op jit(solution)/shard_map/first/pallas_call | solution.py:64
  168.0 18.3 %first.4 = f32[4,3,256,512]{3,2,1,0:T(8,128)} custom-call(s32[8]{0:T(128)} %pad_add_fusion.7.spots, s32[6]{0:T(128)} %pad_add_fusion.6.chips, bf16[6144,3072]{1,0:T(8,128)(2,1)} %t_ref.7, bf16[768,512]{1,0:T(8,128)(2,1)} %collective-permute-done.2.refs_0_, bf16[768,512]{1,0:T(8,128)(2,1)} %collective-permute-done.1.refs_1_, ...), custom_call_target="tpu_custom_call" | custom-call | flops 9663676416 | bytes 25165824 | tf_op jit(solution)/shard_map/first/pallas_call | solution.py:64
  192.8 16.3 %collective-permute-done.8 = bf16[768,512]{1,0:T(8,128)(2,1)S(1)} collective-permute-done((bf16[768,512]{1,0:T(8,128)(2,1)S(1)}, bf16[768,512]{1,0:T(8,128)(2,1)S(1)}, u32[]{:S(2)}, u32[]{:S(2)}) %collective-permute-start.8) | collective-permute-done | bytes 786464 | tf_op jit(solution)/shard_map/ppermute | solution.py:228
  215.8 23.6 %first.6 = f32[4,3,256,768]{3,2,1,0:T(8,128)} custom-call(s32[8]{0:T(128)} %pad_add_fusion.7.spots, s32[6]{0:T(128)} %pad_add_fusion.6.chips, bf16[6144,3072]{1,0:T(8,128)(2,1)} %t_ref.7, bf16[768,768]{1,0:T(8,128)(2,1)} %collective-permute-done.18.refs_0_, bf16[768,768]{1,0:T(8,128)(2,1)} %collective-permute-done.17.refs_1_, bf16[768,768]{1,0:T(8,128)(2,1)} %copy-done.11, ...), custom_call_target="tpu_custom_call" | custom-call | flops 14495514624 | bytes 28311552 | tf_op jit(solution)/shard_map/first/pallas_call | solution.py:64
  265.0 7.3 %collective-permute-done.25 = bf16[128,768]{1,0:T(8,128)(2,1)S(1)} collective-permute-done((bf16[128,768]{1,0:T(8,128)(2,1)S(1)}, bf16[128,768]{1,0:T(8,128)(2,1)S(1)}, u32[]{:S(2)}, u32[]{:S(2)}) %collective-permute-start.25) | collective-permute-done | bytes 196640 | tf_op jit(solution)/shard_map/ppermute | solution.py:228
  294.1 14.7 %collective-permute-done.39.refs_4_ = bf16[768,512]{1,0:T(8,128)(2,1)S(1)} collective-permute-done((bf16[768,512]{1,0:T(8,128)(2,1)S(1)}, bf16[768,512]{1,0:T(8,128)(2,1)S(1)}, u32[]{:S(2)}, u32[]{:S(2)}) %collective-permute-start.39) | collective-permute-done | bytes 786464 | tf_op jit(solution)/shard_map/ppermute | solution.py:224
  309.5 8.0 %collective-permute-done.31 = bf16[768,768]{1,0:T(8,128)(2,1)S(1)} collective-permute-done((bf16[768,768]{1,0:T(8,128)(2,1)S(1)}, bf16[768,768]{1,0:T(8,128)(2,1)S(1)}, u32[]{:S(2)}, u32[]{:S(2)}) %collective-permute-start.31) | collective-permute-done | bytes 1179680 | tf_op jit(solution)/shard_map/ppermute | solution.py:228
  319.4 12.2 %collective-permute-done.11 = bf16[768,512]{1,0:T(8,128)(2,1)S(1)} collective-permute-done((bf16[768,512]{1,0:T(8,128)(2,1)S(1)}, bf16[768,512]{1,0:T(8,128)(2,1)S(1)}, u32[]{:S(2)}, u32[]{:S(2)}) %collective-permute-start.11) | collective-permute-done | bytes 786464 | tf_op jit(solution)/shard_map/ppermute | solution.py:228
  340.0 6.8 %collective-permute-done.33 = bf16[384,768]{1,0:T(8,128)(2,1)S(1)} collective-permute-done((bf16[384,768]{1,0:T(8,128)(2,1)S(1)}, bf16[384,768]{1,0:T(8,128)(2,1)S(1)}, u32[]{:S(2)}, u32[]{:S(2)}) %collective-permute-start.33) | collective-permute-done | bytes 589856 | tf_op jit(solution)/shard_map/ppermute | solution.py:228
  360.5 9.6 %collective-permute-done.65.refs_11_ = bf16[256,768]{1,0:T(8,128)(2,1)S(1)} collective-permute-done((bf16[256,768]{1,0:T(8,128)(2,1)S(1)}, bf16[256,768]{1,0:T(8,128)(2,1)S(1)}, u32[]{:S(2)}, u32[]{:S(2)}) %collective-permute-start.65) | collective-permute-done | bytes 393248 | tf_op jit(solution)/shard_map/ppermute | solution.py:224
  409.2 6.4 %collective-permute-done.56.refs_12_ = bf16[256,768]{1,0:T(8,128)(2,1)} collective-permute-done((bf16[256,768]{1,0:T(8,128)(2,1)S(1)}, bf16[256,768]{1,0:T(8,128)(2,1)}, u32[]{:S(2)}, u32[]{:S(2)}) %collective-permute-start.56) | collective-permute-done | bytes 393248 | tf_op jit(solution)/shard_map/ppermute | solution.py:224
  438.5 8.1 %collective-permute-done.68.refs_3_ = bf16[384,1280]{1,0:T(8,128)(2,1)} collective-permute-done((bf16[384,1280]{1,0:T(8,128)(2,1)}, bf16[384,1280]{1,0:T(8,128)(2,1)}, u32[]{:S(2)}, u32[]{:S(2)}) %collective-permute-start.68) | collective-permute-done | bytes 983072 | tf_op jit(solution)/shard_map/ppermute | solution.py:228
  477.2 13.6 %second.6.refs_9_ = bf16[6144,3072]{1,0:T(8,128)(2,1)} custom-call(s32[2]{0:T(128)} %pad_add_fusion.4.place, s32[6]{0:T(128)} %pad_add_fusion.6.chips, bf16[4,3,256,512]{3,2,1,0:T(8,128)(2,1)} %bitcast.21, bf16[4,3,256,768]{3,2,1,0:T(8,128)(2,1)} %bitcast.12.refs_1_, bf16[256,1280]{1,0:T(8,128)(2,1)} %get-tuple-element.84.refs_2_, ...), custom_call_target="tpu_custom_call" | custom-call | flops 8053063680 | bytes 14155776 | tf_op jit(solution)/shard_map/second/pallas_call | solution.py:132
  497.9 13.2 %collective-permute-done.49.refs_4_ = bf16[384,1280]{1,0:T(8,128)(2,1)} collective-permute-done((bf16[384,1280]{1,0:T(8,128)(2,1)}, bf16[384,1280]{1,0:T(8,128)(2,1)}, u32[]{:S(2)}, u32[]{:S(2)}) %collective-permute-start.49) | collective-permute-done | bytes 983072 | tf_op jit(solution)/shard_map/ppermute | solution.py:228
  514.1 13.6 %second.7.refs_9_ = bf16[6144,3072]{1,0:T(8,128)(2,1)} custom-call(s32[2]{0:T(128)} %pad_add_fusion.5.place, s32[6]{0:T(128)} %pad_add_fusion.6.chips, bf16[4,3,256,512]{3,2,1,0:T(8,128)(2,1)} %bitcast.5.refs_0_, bf16[4,3,256,768]{3,2,1,0:T(8,128)(2,1)} %bitcast.8.refs_1_, ...), custom_call_target="tpu_custom_call", output_to_operand_aliasing={{}: (11, {})} | custom-call | flops 8053063680 | bytes 14155776 | tf_op jit(solution)/shard_map/second/pallas_call | solution.py:132
  527.7 13.6 %second.8.refs_9_ = bf16[6144,3072]{1,0:T(8,128)(2,1)} custom-call(s32[2]{0:T(128)} %pad_add_fusion.2.place, s32[6]{0:T(128)} %pad_add_fusion.6.chips, bf16[4,3,256,512]{3,2,1,0:T(8,128)(2,1)} %bitcast.22, bf16[4,3,256,768]{3,2,1,0:T(8,128)(2,1)} %bitcast.12.refs_1_, bf16[256,1280]{1,0:T(8,128)(2,1)} %get-tuple-element.81.refs_2_, ...), custom_call_target="tpu_custom_call", output_to_operand_aliasing={{}: (11, {})} | custom-call | flops 8053063680 | bytes 14155776 | tf_op jit(solution)/shard_map/second/pallas_call | solution.py:132
  541.3 13.6 %second.9.refs_9_ = bf16[6144,3072]{1,0:T(8,128)(2,1)} custom-call(s32[2]{0:T(128)} %pad_add_fusion.3.place, s32[6]{0:T(128)} %pad_add_fusion.6.chips, bf16[4,3,256,512]{3,2,1,0:T(8,128)(2,1)} %bitcast.5.refs_0_, bf16[4,3,256,768]{3,2,1,0:T(8,128)(2,1)} %bitcast.8.refs_1_, ...), custom_call_target="tpu_custom_call", output_to_operand_aliasing={{}: (11, {})} | custom-call | flops 8053063680 | bytes 14155776 | tf_op jit(solution)/shard_map/second/pallas_call | solution.py:132
  555.7 13.6 %second.10.refs_9_ = bf16[6144,3072]{1,0:T(8,128)(2,1)} custom-call(s32[2]{0:T(128)} %get-tuple-element.117.place, s32[6]{0:T(128)} %pad_add_fusion.6.chips, bf16[4,3,256,512]{3,2,1,0:T(8,128)(2,1)} %bitcast.23, bf16[4,3,256,768]{3,2,1,0:T(8,128)(2,1)} %bitcast.12.refs_1_, ...), custom_call_target="tpu_custom_call", output_to_operand_aliasing={{}: (11, {})} | custom-call | flops 8053063680 | bytes 14155776 | tf_op jit(solution)/shard_map/second/pallas_call | solution.py:132
  569.3 13.6 %second.11 = bf16[6144,3072]{1,0:T(8,128)(2,1)} custom-call(s32[2]{0:T(128)} %get-tuple-element.118.place, s32[6]{0:T(128)} %pad_add_fusion.6.chips, bf16[4,3,256,512]{3,2,1,0:T(8,128)(2,1)} %bitcast.5.refs_0_, bf16[4,3,256,768]{3,2,1,0:T(8,128)(2,1)} %bitcast.8.refs_1_, ...), custom_call_target="tpu_custom_call", output_to_operand_aliasing={{}: (11, {})} | custom-call | flops 8053063680 | bytes 14155776 | tf_op jit(solution)/shard_map/second/pallas_call | solution.py:132
  (254 shorter events, 220.5 us)
Async XLA Ops:
  1.4 30.2 %collective-permute-start.16 = (bf16[768,768]{1,0:T(8,128)(2,1)S(1)}, bf16[768,768]{1,0:T(8,128)(2,1)S(1)}, u32[]{:S(2)}, u32[]{:S(2)}) collective-permute-start(bf16[768,768]{1,0:T(8,128)(2,1)S(1)} %slice.245.refs_3_), channel_id=1, source_target_pairs={{0,1},{1,2},{2,3},{4,5},{5,6},{6,7},{8,9},{9,10},{10,11},{12,13},{... | collective-permute-start | bytes 3538952 | tf_op jit(solution)/shard_map/ppermute | solution.py:223
  6.4 29.3 %collective-permute-start.19 = (bf16[768,768]{1,0:T(8,128)(2,1)S(1)}, bf16[768,768]{1,0:T(8,128)(2,1)S(1)}, u32[]{:S(2)}, u32[]{:S(2)}) collective-permute-start(bf16[768,768]{1,0:T(8,128)(2,1)S(1)} %slice.245.refs_3_), channel_id=1, source_target_pairs={{3,2},{2,1},{1,0},{7,6},{6,5},{5,4},{11,10},{10,9},{9,8},{15,14},{... | collective-permute-start | bytes 3538952 | tf_op jit(solution)/shard_map/ppermute | solution.py:224
  35.7 31.6 %collective-permute-start.20 = (bf16[768,768]{1,0:T(8,128)(2,1)S(1)}, bf16[768,768]{1,0:T(8,128)(2,1)}, u32[]{:S(2)}, u32[]{:S(2)}) collective-permute-start(bf16[768,768]{1,0:T(8,128)(2,1)S(1)} %collective-permute-done.19.refs_4_), channel_id=1, source_target_pairs={{2,1},{1,0},{6,5},{5,4},{10,9},{9,8},{14,13},{13,12},{18,17},{17,1... | collective-permute-start | bytes 3538952 | tf_op jit(solution)/shard_map/ppermute | solution.py:224
  38.2 30.4 %collective-permute-start = (bf16[768,512]{1,0:T(8,128)(2,1)S(1)}, bf16[768,512]{1,0:T(8,128)(2,1)}, u32[]{:S(2)}, u32[]{:S(2)}) collective-permute-start(bf16[768,512]{1,0:T(8,128)(2,1)S(1)} %slice.222.refs_3_), channel_id=1, source_target_pairs={{0,1},{1,2},{2,3},{4,5},{5,6},{6,7},{8,9},{9,10},{10,11},{12,13},{... | collective-permute-start | bytes 2359304 | tf_op jit(solution)/shard_map/ppermute | solution.py:223
  44.5 39.7 %collective-permute-start.3 = (bf16[768,512]{1,0:T(8,128)(2,1)S(1)}, bf16[768,512]{1,0:T(8,128)(2,1)}, u32[]{:S(2)}, u32[]{:S(2)}) collective-permute-start(bf16[768,512]{1,0:T(8,128)(2,1)S(1)} %slice.222.refs_3_), channel_id=1, source_target_pairs={{3,2},{2,1},{1,0},{7,6},{6,5},{5,4},{11,10},{10,9},{9,8},{15,14},{... | collective-permute-start | bytes 2359304 | tf_op jit(solution)/shard_map/ppermute | solution.py:224
  45.8 79.9 %collective-permute-start.18 = (bf16[768,768]{1,0:T(8,128)(2,1)}, bf16[768,768]{1,0:T(8,128)(2,1)}, u32[]{:S(2)}, u32[]{:S(2)}) collective-permute-start(bf16[768,768]{1,0:T(8,128)(2,1)} %collective-permute-done.17.refs_1_), channel_id=1, source_target_pairs={{2,3},{6,7},{10,11},{14,15},{18,19},{22,23},{26,27},{30,31}} | collective-permute-start | bytes 3538952 | tf_op jit(solution)/shard_map/ppermute | solution.py:223
  67.3 58.3 %collective-permute-start.21 = (bf16[768,768]{1,0:T(8,128)(2,1)}, bf16[768,768]{1,0:T(8,128)(2,1)}, u32[]{:S(2)}, u32[]{:S(2)}) collective-permute-start(bf16[768,768]{1,0:T(8,128)(2,1)} %collective-permute-done.20.refs_5_), channel_id=1, source_target_pairs={{1,0},{5,4},{9,8},{13,12},{17,16},{21,20},{25,24},{29,28}} | collective-permute-start | bytes 3538952 | tf_op jit(solution)/shard_map/ppermute | solution.py:224
  84.2 40.1 %collective-permute-start.4 = (bf16[768,512]{1,0:T(8,128)(2,1)}, bf16[768,512]{1,0:T(8,128)(2,1)}, u32[]{:S(2)}, u32[]{:S(2)}) collective-permute-start(bf16[768,512]{1,0:T(8,128)(2,1)} %collective-permute-done.3.refs_4_), channel_id=1, source_target_pairs={{2,1},{1,0},{6,5},{5,4},{10,9},{9,8},{14,13},{13,12},{18,17},{17,1... | collective-permute-start | bytes 2359304 | tf_op jit(solution)/shard_map/ppermute | solution.py:224
  86.8 62.4 %collective-permute-start.2 = (bf16[768,512]{1,0:T(8,128)(2,1)}, bf16[768,512]{1,0:T(8,128)(2,1)}, u32[]{:S(2)}, u32[]{:S(2)}) collective-permute-start(bf16[768,512]{1,0:T(8,128)(2,1)} %collective-permute-done.1.refs_1_), channel_id=1, source_target_pairs={{2,3},{6,7},{10,11},{14,15},{18,19},{22,23},{26,27},{30,31}} | collective-permute-start | bytes 2359304 | tf_op jit(solution)/shard_map/ppermute | solution.py:223
  149.2 90.2 %collective-permute-start.22 = (f32[3072,768]{1,0:T(8,128)}, f32[3072,768]{1,0:T(8,128)}, u32[]{:S(2)}, u32[]{:S(2)}) collective-permute-start(f32[3072,768]{1,0:T(8,128)} %bitcast.28), channel_id=1, source_target_pairs={{0,4},{4,0},{8,12},{12,8},{16,20},{20,16},{24,28},{28,24},{1,5},{5... | collective-permute-start | bytes 28311560 | tf_op jit(solution)/shard_map/ppermute | solution.py:231
  259.3 33.2 %collective-permute-start.36 = (bf16[768,512]{1,0:T(8,128)(2,1)S(1)}, bf16[768,512]{1,0:T(8,128)(2,1)S(1)}, u32[]{:S(2)}, u32[]{:S(2)}) collective-permute-start(bf16[768,512]{1,0:T(8,128)(2,1)S(1)} %pad_maximum_fusion.3.refs_3_), channel_id=1, source_target_pairs={{0,1},{1,2},{2,3},{4,5},{5,6},{6,7},{8,9},{9,10},{10,11},{12,13},{... | collective-permute-start | bytes 2359304 | tf_op jit(solution)/shard_map/ppermute | solution.py:223
  289.2 29.7 %collective-permute-start.32 = (bf16[768,768]{1,0:T(8,128)(2,1)S(1)}, bf16[768,768]{1,0:T(8,128)(2,1)S(1)}, u32[]{:S(2)}, u32[]{:S(2)}) collective-permute-start(bf16[768,768]{1,0:T(8,128)(2,1)S(1)} %pad_maximum_fusion), channel_id=1, source_target_pairs={{0,16},{4,20},{8,24},{12,28},{16,0},{20,4},{24,8},{28,12},{1,17},{... | collective-permute-start | bytes 3538952 | tf_op jit(solution)/shard_map/ppermute | solution.py:228
  291.1 40.5 %collective-permute-start.11 = (bf16[768,512]{1,0:T(8,128)(2,1)S(1)}, bf16[768,512]{1,0:T(8,128)(2,1)S(1)}, u32[]{:S(2)}, u32[]{:S(2)}) collective-permute-start(bf16[768,512]{1,0:T(8,128)(2,1)S(1)} %pad_maximum_fusion.3.refs_3_), channel_id=1, source_target_pairs={{0,8},{4,12},{8,0},{12,4},{16,24},{20,28},{24,16},{28,20},{1,9},{5... | collective-permute-start | bytes 2359304 | tf_op jit(solution)/shard_map/ppermute | solution.py:228
  292.5 42.4 %collective-permute-start.12 = (bf16[768,512]{1,0:T(8,128)(2,1)S(1)}, bf16[768,512]{1,0:T(8,128)(2,1)S(1)}, u32[]{:S(2)}, u32[]{:S(2)}) collective-permute-start(bf16[768,512]{1,0:T(8,128)(2,1)S(1)} %pad_maximum_fusion.3.refs_3_), channel_id=1, source_target_pairs={{0,16},{4,20},{8,24},{12,28},{16,0},{20,4},{24,8},{28,12},{1,17},{... | collective-permute-start | bytes 2359304 | tf_op jit(solution)/shard_map/ppermute | solution.py:228
  339.3 32.1 %collective-permute-start.38 = (bf16[768,512]{1,0:T(8,128)(2,1)S(1)}, bf16[768,512]{1,0:T(8,128)(2,1)S(1)}, u32[]{:S(2)}, u32[]{:S(2)}) collective-permute-start(bf16[768,512]{1,0:T(8,128)(2,1)S(1)} %collective-permute-done.37.refs_1_), channel_id=1, source_target_pairs={{2,3},{6,7},{10,11},{14,15},{18,19},{22,23},{26,27},{30,31}} | collective-permute-start | bytes 2359304 | tf_op jit(solution)/shard_map/ppermute | solution.py:223
  346.8 29.2 %collective-permute-start.41 = (bf16[768,512]{1,0:T(8,128)(2,1)S(1)}, bf16[768,512]{1,0:T(8,128)(2,1)S(1)}, u32[]{:S(2)}, u32[]{:S(2)}) collective-permute-start(bf16[768,512]{1,0:T(8,128)(2,1)S(1)} %collective-permute-done.40.refs_5_), channel_id=1, source_target_pairs={{1,0},{5,4},{9,8},{13,12},{17,16},{21,20},{25,24},{29,28}} | collective-permute-start | bytes 2359304 | tf_op jit(solution)/shard_map/ppermute | solution.py:224
  355.4 158.7 %collective-permute-start.35 = (bf16[3072,768]{1,0:T(8,128)(2,1)}, bf16[3072,768]{1,0:T(8,128)(2,1)}, u32[]{:S(2)}, u32[]{:S(2)}) collective-permute-start(bf16[3072,768]{1,0:T(8,128)(2,1)} %constant_dynamic-update-slice_fusion.6), channel_id=1, source_target_pairs={{0,4},{4,0},{8,12},{12,8},{16,20},{20,16},{24,28},{28,24},{1,5},{5... | collective-permute-start | bytes 14155784 | tf_op jit(solution)/shard_map/ppermute | solution.py:231
  409.2 104.2 %collective-permute-start.15 = (bf16[3072,512]{1,0:T(8,128)(2,1)S(1)}, bf16[3072,512]{1,0:T(8,128)(2,1)}, u32[]{:S(2)}, u32[]{:S(2)}) collective-permute-start(bf16[3072,512]{1,0:T(8,128)(2,1)S(1)} %constant_dynamic-update-slice_fusion), channel_id=1, source_target_pairs={{0,4},{4,0},{8,12},{12,8},{16,20},{20,16},{24,28},{28,24},{1,5},{5... | collective-permute-start | bytes 9437192 | tf_op jit(solution)/shard_map/ppermute | solution.py:231
  437.1 36.2 %collective-permute-start.58 = (bf16[384,1280]{1,0:T(8,128)(2,1)}, bf16[384,1280]{1,0:T(8,128)(2,1)}, u32[]{:S(2)}, u32[]{:S(2)}) collective-permute-start(bf16[384,1280]{1,0:T(8,128)(2,1)} %get-tuple-element.82), channel_id=1, source_target_pairs={{0,8},{4,12},{8,0},{12,4},{16,24},{20,28},{24,16},{28,20},{1,9},{5... | collective-permute-start | bytes 2949128 | tf_op jit(solution)/shard_map/ppermute | solution.py:228
  473.3 37.8 %collective-permute-start.49 = (bf16[384,1280]{1,0:T(8,128)(2,1)}, bf16[384,1280]{1,0:T(8,128)(2,1)}, u32[]{:S(2)}, u32[]{:S(2)}) collective-permute-start(bf16[384,1280]{1,0:T(8,128)(2,1)} %get-tuple-element.80), channel_id=1, source_target_pairs={{0,16},{4,20},{8,24},{12,28},{16,0},{20,4},{24,8},{28,12},{1,17},{... | collective-permute-start | bytes 2949128 | tf_op jit(solution)/shard_map/ppermute | solution.py:228
  492.5 35.2 %collective-permute-start.60 = (bf16[128,1280]{1,0:T(8,128)(2,1)}, bf16[128,1280]{1,0:T(8,128)(2,1)}, u32[]{:S(2)}, u32[]{:S(2)}) collective-permute-start(bf16[128,1280]{1,0:T(8,128)(2,1)} %slice.318), channel_id=1, source_target_pairs={{0,16},{4,20},{8,24},{12,28},{16,0},{20,4},{24,8},{28,12},{1,17},{... | collective-permute-start | bytes 983048 | tf_op jit(solution)/shard_map/ppermute | solution.py:228
  495.6 32.0 %collective-permute-start.61 = (bf16[128,1280]{1,0:T(8,128)(2,1)}, bf16[128,1280]{1,0:T(8,128)(2,1)}, u32[]{:S(2)}, u32[]{:S(2)}) collective-permute-start(bf16[128,1280]{1,0:T(8,128)(2,1)} %slice.319), channel_id=1, source_target_pairs={{0,8},{4,12},{8,0},{12,4},{16,24},{20,28},{24,16},{28,20},{1,9},{5... | collective-permute-start | bytes 983048 | tf_op jit(solution)/shard_map/ppermute | solution.py:228
  511.1 43.7 %collective-permute-start.50 = (bf16[128,1280]{1,0:T(8,128)(2,1)}, bf16[128,1280]{1,0:T(8,128)(2,1)S(1)}, u32[]{:S(2)}, u32[]{:S(2)}) collective-permute-start(bf16[128,1280]{1,0:T(8,128)(2,1)} %slice.316), channel_id=1, source_target_pairs={{0,16},{4,20},{8,24},{12,28},{16,0},{20,4},{24,8},{28,12},{1,17},{... | collective-permute-start | bytes 983048 | tf_op jit(solution)/shard_map/ppermute | solution.py:228
  513.4 41.5 %collective-permute-start.51 = (bf16[128,1280]{1,0:T(8,128)(2,1)}, bf16[128,1280]{1,0:T(8,128)(2,1)S(1)}, u32[]{:S(2)}, u32[]{:S(2)}) collective-permute-start(bf16[128,1280]{1,0:T(8,128)(2,1)} %slice.317), channel_id=1, source_target_pairs={{0,8},{4,12},{8,0},{12,4},{16,24},{20,28},{24,16},{28,20},{1,9},{5... | collective-permute-start | bytes 983048 | tf_op jit(solution)/shard_map/ppermute | solution.py:228
  (82 other events, 2126.4 us)
